TPU v7x, 32 devices: a whole 2x2x4 slice. The times are simulated.
32 devices in a mesh: row: 4 (over x, core), col: 2 (over y), date: 4 (over z).
Axes of the slice: x: 2, y: 2, z: 4, core: 2. Of those that a mesh axis runs over, the one named last changes fastest.
Arguments:
- slc: bfloat16 [2, 48, 24, 512], P(None, 'date', 'row', 'col'), may hold values from -6 to 6
- pairs: int32 [32, 2], P('date'), may hold values from 0 to 47, as said below
- target: float32 [2, 32, 12, 128], P(None, 'date', 'row', 'col'), may hold values from -4 to 4
- w_lift: bfloat16 [2, 3, 3, 64], replicated, may hold values from -1.5 to 1.5
- b_lift: bfloat16 [2, 64], replicated, may hold values from -2 to 2
- w_mid: bfloat16 [2, 3, 3, 64, 64], replicated, may hold values from -0.1875 to 0.1875
- b_mid: bfloat16 [2, 64], replicated, may hold values from -2 to 2
- w_proj: bfloat16 [2, 3, 3, 64], replicated, may hold values from -0.1875 to 0.1875
Outputs:
- denoised: float32 [2, 32, 12, 128], P(None, 'date', 'row', 'col')
- grad_lift: float32 [2, 3, 3, 64], replicated
- grad_lift_bias: float32 [2, 64], replicated
- grad_mid: float32 [2, 3, 3, 64, 64], replicated
- grad_mid_bias: float32 [2, 64], replicated
- grad_proj: float32 [2, 3, 3, 64], replicated
Inputs may be any that keep to these rules, and one draw needn't show every extreme that they name: `pairs`: row p belongs to date index p // 8, which holds dates d * 12 to (d + 1) * 12 - 1; its earlier date lies there, and its later date is later by 1 to 24 dates. Row 0 is (0, 24).
All inputs are finite; a program needn't handle non-finite values.
Results may differ from a plain program's by a relative error of at most 0.00065.
The roundings to bfloat16 on the way count: a program that leaves them out, or rounds other values in their place, can miss the bound.
Values may be sent and summed in bfloat16 or wider, within the bound.
A program may use at most 64 MiB of HBM per device.

v0:
```python
import functools
import math

import jax
import jax.numpy as jnp
from jax import lax
from jax.experimental import pallas as pl
from jax.experimental.pallas import tpu as pltpu
from jax.sharding import PartitionSpec as P

MESH = pl.DeviceIdType.MESH

LR = 2
LC = 4


def mm(a, b):
    return jnp.dot(a, b, preferred_element_type=jnp.float32)


def mm_t(a, b):
    return lax.dot_general(a, b, (((1,), (1,)), ((), ())), preferred_element_type=jnp.float32)


def step_kernel(
    dims, scale,
    slc_ref, pick_ref, avg_ref, tgt_ref, wl_any, bl_any, wmid_any, bmid_any, wproj_any,
    den_ref, o_ref, small_ref,
    pool, look_f, look_s, look_r, tgt_r, fld, tfld, i3a, i3b, h2s, tsum, dn3, dnm3, dp2m, dp1, outs, x_ref,
    wl_in, bl_in, wm_in, bm_in, wj_in, w_sem, w1_ref, wp_ref, wpb_ref, wf_ref, wb_ref, bm_ref, wtmp,
    plane_in, date_in, small_in, small_date, small_sem, small_date_sem, slab_sem, look_sem, tgt_sem, den_sem, plane_sem, date_sem, gather_sem,
):
    n_row, n_col, n_date, pp, tr, tc = dims
    r, c, d = lax.axis_index("row"), lax.axis_index("col"), lax.axis_index("date")
    n_plane = n_row * n_col
    me = r * n_col + c
    rows = n_row * tr
    gap = rows + 1
    nb = gap * pp
    n = nb * 128
    base = (128 - tc) // 2
    pairs = pp * n_row
    f32, bf16 = jnp.float32, jnp.bfloat16

    def plane_peer(k):
        peer = lax.rem(me + k, n_plane)
        return peer, (lax.div(peer, n_col), lax.rem(peer, n_col), d)

    def date_peer(k):
        return (r, c, lax.rem(d + k, n_date))

    def remote(src, dst, sems, at, where):
        copy = pltpu.make_async_remote_copy(
            src_ref=src, dst_ref=dst, send_sem=sems.at[0, at], recv_sem=sems.at[1, at],
            device_id=where, device_id_type=MESH,
        )
        copy.start()
        return copy

    fetches = []
    wide = zip((wl_any, bl_any, wmid_any, bmid_any, wproj_any), (wl_in, bl_in, wm_in, bm_in, wj_in))
    for k, (src, dst) in enumerate(wide):
        copy = pltpu.make_async_copy(src, dst, w_sem.at[k])
        copy.start()
        fetches.append(copy)
    barrier = pltpu.get_barrier_semaphore()
    for k in range(1, n_plane):
        pl.semaphore_signal(barrier, inc=1, device_id=plane_peer(k)[1], device_id_type=MESH)
    for k in range(1, n_date):
        pl.semaphore_signal(barrier, inc=1, device_id=date_peer(k), device_id_type=MESH)
    pl.semaphore_wait(barrier, n_plane + n_date - 2)

    sent = []
    slabs = [remote(slc_ref, pool.at[k - 1], slab_sem, k, date_peer(n_date - k)) for k in (1, 2)]

    def exchange(src, dst, sems):
        copies = []
        for way in range(3):
            col = lax.rem(c + (0, 1, n_col - 1)[way], n_col)
            for o in range(n_row):
                k = lax.rem(r + o, n_row)
                at = way * n_row + o
                if way == 0 and o == 0:
                    copy = pltpu.make_async_copy(src.at[k], dst.at[0, r], sems.at[0, at])
                    copy.start()
                    copies.append((copy, True))
                else:
                    copies.append((remote(src.at[k], dst.at[way, r], sems, at, (k, col, d)), False))
        return copies

    tgt_copies = exchange(tgt_ref, tgt_r, tgt_sem)
    for ref in (fld, tfld, dn3, dnm3, tsum):
        ref[...] = jnp.zeros_like(ref)
    edge = jnp.zeros((i3a.shape[0], 128), bf16)
    for ref in (i3a, i3b):
        ref[:, 0:128] = edge
        ref[:, (nb + 1) * 128 : (nb + 2) * 128] = edge
    x_ref[...] = jnp.zeros_like(x_ref)
    lane = lax.broadcasted_iota(jnp.int32, (1, 128), 1)
    spot = c * tc + lane - base
    inside = (spot >= 0) & (spot < n_col * tc)
    own = (lane >= base) & (lane < base + tc)
    for copy in fetches:
        copy.wait()
    wtmp[...] = jnp.zeros_like(wtmp)

    def joined(a, b):
        return jnp.concatenate([a, b], axis=1)

    for t in range(3):
        for u in range(3):
            pair = wl_in[t, u].astype(f32)
            at = 8 * t + 2 * u
            wtmp[0, at : at + 1, :] = joined(pair[0:1], pair[1:2])
            wtmp[0, at + 1 : at + 2, :] = joined(-pair[1:2], pair[0:1])
            pair = wj_in[t, u].astype(f32)
            real, imag = joined(pair[0:1], -pair[1:2]), joined(pair[1:2], pair[0:1])
            flip = 8 * (2 - t) + 2 * (2 - u)
            wtmp[1, at : at + 1, :] = real
            wtmp[1, at + 1 : at + 2, :] = imag
            wtmp[2, flip : flip + 1, :] = real
            wtmp[2, flip + 1 : flip + 2, :] = imag
            wr, wi = wm_in[0, t, u].astype(f32), wm_in[1, t, u].astype(f32)
            block = jnp.concatenate([joined(wr, wi), joined(-wi, wr)], axis=0)
            wb_ref[2 - t, :, (2 - u) * 128 : (3 - u) * 128] = block.astype(bf16)
            wf_ref[t, :, u * 128 : (u + 1) * 128] = block.T.astype(bf16)
    bias = bl_in[...].astype(f32)
    wtmp[0, 14:15, :] = joined(bias[0:1], bias[1:2])
    bias = bm_in[...].astype(f32)
    wtmp[3, 0:1, :] = joined(bias[0:1], bias[1:2])
    w1_ref[...] = wtmp[0].T[:, 0:32].astype(bf16)
    wp_ref[...] = wtmp[1, 0:32].astype(bf16)
    wpb_ref[...] = wtmp[2].T[:, 0:32].astype(bf16)
    bm_ref[...] = wtmp[3].T[:, 0:1]
    for copy in slabs:
        copy.wait_recv()
    sent += slabs

    depth = slc_ref.shape[0]
    picked = (
        mm(pick_ref[:, :depth], slc_ref[...])
        + mm(pick_ref[:, depth : 2 * depth], pool[0])
        + mm(pick_ref[:, 2 * depth :], pool[1])
    )
    parts = slc_ref.shape[1] // (LR * tr)
    halves = tc * LC // parts
    sides = []
    for h in range(halves):
        at = [picked[q * pairs : (q + 1) * pairs] for q in (h, halves + h, 2 * halves + h, 3 * halves + h)]
        a0, a1, b0, b1 = at
        rowsum = []
        for prod in (a0 * b0 + a1 * b1, a1 * b0 - a0 * b1):
            for t in range(tr):
                rowsum.append(
                    sum(prod[:, (t * LR + q) * parts : (t * LR + q + 1) * parts] for q in range(LR))
                )
        sides.append(jnp.concatenate(rowsum, axis=0))
    looked = jnp.dot(
        jnp.concatenate(sides, axis=1), avg_ref[...],
        precision=lax.Precision.HIGHEST, preferred_element_type=f32,
    )
    look_f[...] = jnp.zeros_like(look_f)
    for k in range(n_row):
        for q in range(2 * tr):
            look_f[k, q * pp : (q + 1) * pp, :] = looked[q * pairs + k * pp : q * pairs + (k + 1) * pp]
    look_s[...] = look_f[...].astype(bf16)
    look_copies = exchange(look_s, look_r, look_sem)

    def settle(copies):
        for copy, near in copies:
            if near:
                copy.wait()
            else:
                copy.wait_recv()
                sent.append(copy)

    def assemble(ref, s):
        mid = pltpu.roll(ref[0, s].astype(f32), base, 1)
        low = pltpu.roll(ref[1, s].astype(f32), (base - tc) % 128, 1)
        high = pltpu.roll(ref[2, s].astype(f32), base + tc, 1)
        joined = jnp.where(own, mid, jnp.where(lane < base, low, high))
        near = (lane >= base - 5) & (lane < base + tc + 5)
        return jnp.where(inside & near, joined, 0.0)

    settle(tgt_copies)
    for s in range(n_row):
        block = assemble(tgt_r, s)
        for z in range(2):
            for t in range(tr):
                for p in range(pp):
                    i = (z * tr + t) * pp + p
                    b = p * gap + s * tr + t
                    tfld[z : z + 1, b * 128 : (b + 1) * 128] = block[i : i + 1]
    settle(look_copies)
    for s in range(n_row):
        block = assemble(look_r, s)
        for u, turned in enumerate((pltpu.roll(block, 1, 1), block, pltpu.roll(block, 127, 1))):
            for z in range(2):
                for t in range(tr):
                    for p in range(pp):
                        i = (z * tr + t) * pp + p
                        b = p * gap + s * tr + t + 1
                        fld[2 * u + z : 2 * u + z + 1, b * 128 : (b + 1) * 128] = turned[i : i + 1]
    fld[6:7, :] = jnp.ones((1, (nb + 2) * 128), f32)

    def taps(ref, at, width):
        three = [ref[:, pl.ds(pl.multiple_of(at + t * 128, 128), width)] for t in range(3)]
        return jnp.concatenate(three + [jnp.zeros((8, width), f32)], axis=0).astype(bf16)

    def turned_store(ref, value, at):
        for u, turn in enumerate((1, 0, 127)):
            for q in range(2):
                piece = value[:, q * 128 : (q + 1) * 128]
                if turn:
                    piece = pltpu.roll(piece, turn, 1)
                ref[u * 128 : (u + 1) * 128, pl.ds(pl.multiple_of(at + (q + 1) * 128, 128), 128)] = (
                    piece.astype(bf16)
                )

    def good(b):
        one = [inside & (lax.rem(b + q, gap) != gap - 1) for q in range(2)]
        return jnp.concatenate(one, axis=1)

    own2 = jnp.concatenate([own, own], axis=1)

    def rounded(value):
        return value.astype(bf16).astype(f32)

    def lift(i, carry):
        at = pl.multiple_of(i * 256, 256)
        pre1 = mm(w1_ref[...], taps(fld, at, 256))
        turned_store(i3a, rounded(jnp.where(good(2 * i), jnp.maximum(pre1, 0.0), 0.0)), at)
        return carry

    lax.fori_loop(0, nb // 2, lift, 0, unroll=True)

    def conv(w_ref, ref, at):
        total = 0.0
        for t in range(3):
            total = total + mm(w_ref[t], ref[:, pl.ds(pl.multiple_of(at + t * 128, 128), 256)])
        return total

    def mid(i, carry):
        at = pl.multiple_of(i * 256, 256)
        pre2 = conv(wf_ref, i3a, at) + bm_ref[...]
        h2 = jnp.where(good(2 * i), jnp.maximum(pre2, 0.0), 0.0).astype(bf16)
        h2s[:, pl.ds(at, 256)] = h2
        tsum[:, pl.ds(pl.multiple_of(at + 128, 128), 256)] = mm(wp_ref[...], h2)
        return carry

    lax.fori_loop(0, nb // 2, mid, 0, unroll=True)

    six = sum(tsum[8 * t : 8 * t + 8, t * 128 : t * 128 + n] for t in range(3))
    noise = pltpu.roll(six, 1, 1)[0:2] + six[2:4] + pltpu.roll(six, n - 1, 1)[4:6]
    den = fld[2:4, 128 : 128 + n] - noise
    shifted = pltpu.roll(den, n - base, 1)
    outs[...] = jnp.zeros_like(outs)
    for s in range(n_row):
        for z in range(2):
            for t in range(tr):
                for p in range(pp):
                    i = (z * tr + t) * pp + p
                    b = p * gap + s * tr + t
                    outs[s, i : i + 1, :] = shifted[z : z + 1, b * 128 : (b + 1) * 128]
    den_copies = []
    for o in range(n_row):
        k = lax.rem(r + o, n_row)
        if o == 0:
            copy = pltpu.make_async_copy(outs.at[k], den_ref.at[r], den_sem.at[0, o])
            copy.start()
            den_copies.append((copy, True))
        else:
            den_copies.append((remote(outs.at[k], den_ref.at[r], den_sem, o, (k, c, d)), False))
    dn = rounded((tfld[0:2, :] - den) * scale)
    rowok = [jnp.full((1, 128), b % gap != gap - 1) for b in range(nb)]
    mask = jnp.concatenate([inside & ok for ok in rowok], axis=1)
    own_all = jnp.concatenate([own & ok for ok in rowok], axis=1)
    for ref, keep in ((dn3, mask), (dnm3, own_all)):
        kept = jnp.where(keep, dn, 0.0)
        ref[0:2, 128 : 128 + n] = pltpu.roll(kept, 1, 1)
        ref[2:4, 128 : 128 + n] = kept
        ref[4:6, 128 : 128 + n] = pltpu.roll(kept, n - 1, 1)

    def back2(i, carry):
        at = pl.multiple_of(i * 256, 256)
        grad = mm(wpb_ref[...], taps(dn3, at, 256))
        grad = rounded(jnp.where(h2s[:, pl.ds(at, 256)].astype(f32) > 0, grad, 0.0))
        turned_store(i3b, grad, at)
        dp2m[:, pl.ds(at, 256)] = jnp.where(own2, grad, 0.0).astype(bf16)
        return carry

    lax.fori_loop(0, nb // 2, back2, 0, unroll=True)

    sign = jnp.where(lane < 64, 1.0, -1.0)
    for t in range(3):
        gram = mm_t(i3a[:, t * 128 : t * 128 + n], dp2m[...])
        for u in range(3):
            upper = gram[u * 128 : u * 128 + 64]
            lower = gram[u * 128 + 64 : u * 128 + 128]
            x_ref[(3 * t + u) * 64 : (3 * t + u) * 64 + 64, :] = upper + sign * pltpu.roll(lower, 64, 1)
    x_ref[576:600, :] = mm_t(taps(dnm3, 0, n), h2s[...])[0:24]
    x_ref[600:608, :] = mm_t(jnp.ones((16, n), bf16), dp2m[...])[0:8]

    piece = plane_in.shape[1]

    def slot(ref, k):
        return ref.at[pl.ds(pl.multiple_of(k * piece, 8), piece)]

    scatter = []
    for k in range(1, n_plane):
        peer, where = plane_peer(k)
        scatter.append(remote(slot(x_ref, peer), plane_in.at[k], plane_sem, k, where))

    def back1(i, carry):
        at = pl.multiple_of(i * 256, 256)
        h1 = i3a[128:256, pl.ds(pl.multiple_of(at + 128, 128), 256)].astype(f32)
        grad = jnp.where((h1 > 0) & own2, conv(wb_ref, i3b, at), 0.0)
        dp1[:, pl.ds(at, 256)] = grad.astype(bf16)
        return carry

    lax.fori_loop(0, nb // 2, back1, 0, unroll=True)

    small_in[me] = mm_t(taps(fld, 0, n), dp1[...])[0:24]
    small = [
        remote(small_in.at[me], small_in.at[me], small_sem, k, plane_peer(k)[1]) for k in range(1, n_plane)
    ]
    part = slot(x_ref, me)[...]
    for k, copy in zip(range(1, n_plane), scatter):
        copy.wait_recv()
        part = part + plane_in[k]
    date_in[d] = part
    spread = [remote(date_in.at[d], date_in.at[d], date_sem, k, date_peer(k)) for k in range(1, n_date)]

    def total(ref, count):
        return functools.reduce(lambda a, b: a + b, [ref[k] for k in range(count)])

    for copy in small:
        copy.wait_recv()
    small_date[d] = total(small_in, n_plane)
    small_spread = [
        remote(small_date.at[d], small_date.at[d], small_date_sem, k, date_peer(k)) for k in range(1, n_date)
    ]
    for copy in spread:
        copy.wait_recv()
    slot(o_ref, me)[...] = total(date_in, n_date)
    gather = [
        remote(slot(o_ref, me), slot(o_ref, me), gather_sem, k, plane_peer(k)[1])
        for k in range(1, n_plane)
    ]
    for copy in small_spread:
        copy.wait_recv()
    small_ref[...] = total(small_date, n_date)
    settle(den_copies)
    for copy in gather:
        copy.wait_recv()
    for copy in sent + scatter + small + spread + small_spread + gather:
        copy.wait_send()


def finish_kernel(dims, den, sums, small, den_out, lift_out, lbias_out, mid_out, mbias_out, proj_out):
    n_row, pp, tr, tc, ch = dims
    for k in range(n_row):
        for z in range(2):
            for t in range(tr):
                at = (z * tr + t) * pp
                den_out[z, t, k * pp : (k + 1) * pp, :] = den[k, at : at + pp, 0:tc]
    for t in range(3):
        for u in range(3):
            at = 8 * t + 2 * u
            upper, lower = small[at : at + 1, :], small[at + 1 : at + 2, :]
            lift_out[t, u, 0:1, :] = upper[:, 0:ch] + lower[:, ch:]
            lift_out[t, u, 1:2, :] = upper[:, ch:] - lower[:, 0:ch]
            at = 576 + 8 * (2 - t) + 2 * (2 - u)
            upper, lower = sums[at : at + 1, :], sums[at + 1 : at + 2, :]
            proj_out[t, u, 0:1, :] = upper[:, 0:ch] + lower[:, ch:]
            proj_out[t, u, 1:2, :] = lower[:, 0:ch] - upper[:, ch:]
            at = (3 * t + u) * ch
            for z in range(2):
                mid_out[z, t, u] = sums[at : at + ch, z * ch : (z + 1) * ch]
    for z in range(2):
        lbias_out[z : z + 1, :] = small[14:15, z * ch : (z + 1) * ch]
        mbias_out[z : z + 1, :] = sums[600:601, z * ch : (z + 1) * ch]


def local(slc, pairs, target, w_lift, b_lift, w_mid, b_mid, w_proj):
    n_row, n_col, n_date = (lax.axis_size(axis) for axis in ("row", "col", "date"))
    dates, srows, scols = slc.shape[1:]
    count, tr, tc = target.shape[1:]
    ch = w_mid.shape[-1]
    pp = count // n_row
    halves = scols // 128
    bf16, f32 = jnp.bfloat16, jnp.float32
    rows = 2 * tr * pp
    pad_rows = -(-rows // 16) * 16
    packed = slc.reshape(2, dates, srows, halves, 128).transpose(1, 0, 3, 2, 4)
    packed = packed.reshape(dates * 2 * halves, srows * 128)
    index = (pairs - lax.axis_index("date") * dates).T
    kinds = 2 * halves
    want = (index[:, None, :] * kinds + jnp.arange(kinds, dtype=jnp.int32)[None, :, None]).reshape(-1)
    pick = (want[:, None] == jnp.arange(3 * dates * kinds, dtype=jnp.int32)[None, :]).astype(bf16)
    spots = jnp.arange(scols, dtype=jnp.int32)[:, None] // LC
    avg = jnp.where(spots == jnp.arange(128, dtype=jnp.int32)[None, :], 1.0 / (LR * LC), 0.0).astype(f32)
    tgt = target.reshape(2, n_row, pp, tr, tc).transpose(1, 0, 3, 2, 4).reshape(n_row, rows, tc)
    tgt = jnp.pad(tgt, ((0, 0), (0, pad_rows - rows), (0, 128 - tc)))
    w_lift, w_proj = w_lift.transpose(1, 2, 0, 3), w_proj.transpose(1, 2, 0, 3)
    scale = 1.0 / math.sqrt(2.0 * count * n_date * tr * n_row * tc * n_col)
    nb = (n_row * tr + 1) * pp
    n, wide = nb * 128, (nb + 2) * 128
    n_plane = n_row * n_col
    piece = -(-608 // (8 * n_plane)) * 8
    dma = pltpu.SemaphoreType.DMA
    vmem = pltpu.VMEM
    den, sums, small = pl.pallas_call(
        functools.partial(step_kernel, (n_row, n_col, n_date, pp, tr, tc), scale),
        out_shape=(
            jax.ShapeDtypeStruct((n_row, pad_rows, 128), f32),
            jax.ShapeDtypeStruct((n_plane * piece, 128), f32),
            jax.ShapeDtypeStruct((24, 128), f32),
        ),
        in_specs=[pl.BlockSpec(memory_space=vmem)] * 4 + [pl.BlockSpec(memory_space=pl.ANY)] * 5,
        out_specs=(pl.BlockSpec(memory_space=vmem),) * 3,
        scratch_shapes=[
            vmem((2,) + packed.shape, bf16),
            vmem((n_row, pad_rows, 128), f32),
            vmem((n_row, pad_rows, 128), bf16),
            vmem((3, n_row, pad_rows, 128), bf16),
            vmem((3, n_row, pad_rows, 128), f32),
            vmem((8, wide), f32),
            vmem((8, n), f32),
            vmem((6 * ch, wide), bf16),
            vmem((6 * ch, wide), bf16),
            vmem((2 * ch, n), bf16),
            vmem((32, wide), f32),
            vmem((8, wide), f32),
            vmem((8, wide), f32),
            vmem((2 * ch, n), bf16),
            vmem((2 * ch, n), bf16),
            vmem((n_row, pad_rows, 128), f32),
            vmem((n_plane * piece, 128), f32),
            vmem(w_lift.shape, bf16),
            vmem(b_lift.shape, bf16),
            vmem(w_mid.shape, bf16),
            vmem(b_mid.shape, bf16),
            vmem(w_proj.shape, bf16),
            dma((5,)),
            vmem((2 * ch, 32), bf16),
            vmem((32, 2 * ch), bf16),
            vmem((2 * ch, 32), bf16),
            vmem((3, 2 * ch, 6 * ch), bf16),
            vmem((3, 2 * ch, 6 * ch), bf16),
            vmem((2 * ch, 1), f32),
            vmem((4, 128, 128), f32),
            vmem((n_plane, piece, 128), f32),
            vmem((n_date, piece, 128), f32),
            vmem((n_plane, 24, 128), f32),
            vmem((n_date, 24, 128), f32),
            dma((2, n_plane)),
            dma((2, n_date)),
            dma((2, 3)),
            dma((2, 3 * n_row)),
            dma((2, 3 * n_row)),
            dma((2, n_row)),
            dma((2, n_plane)),
            dma((2, n_date)),
            dma((2, n_plane)),
        ],
        compiler_params=pltpu.CompilerParams(
            collective_id=0, has_side_effects=True, vmem_limit_bytes=48 * 1024 * 1024
        ),
    )(packed, pick, avg, tgt, w_lift, b_lift, w_mid, b_mid, w_proj)
    shape = jax.ShapeDtypeStruct
    denoised, grad_lift, lift_bias, grad_mid, mid_bias, grad_proj = pl.pallas_call(
        functools.partial(finish_kernel, (n_row, pp, tr, tc, ch)),
        out_shape=(
            shape((2, tr, count, tc), f32),
            shape((3, 3, 2, ch), f32),
            shape((2, ch), f32),
            shape((2, 3, 3, ch, ch), f32),
            shape((2, ch), f32),
            shape((3, 3, 2, ch), f32),
        ),
        in_specs=[pl.BlockSpec(memory_space=vmem)] * 3,
        out_specs=(pl.BlockSpec(memory_space=vmem),) * 6,
        compiler_params=pltpu.CompilerParams(vmem_limit_bytes=8 * 1024 * 1024),
    )(den, sums, small)
    return (
        denoised.transpose(0, 2, 1, 3),
        grad_lift.transpose(2, 0, 1, 3),
        lift_bias,
        grad_mid,
        mid_bias,
        grad_proj.transpose(2, 0, 1, 3),
    )


def solution(mesh):
    in_specs = (
        P(None, "date", "row", "col"),
        P("date", None),
        P(None, "date", "row", "col"),
        P(),
        P(),
        P(),
        P(),
        P(),
    )
    out_specs = (P(None, "date", "row", "col"), P(), P(), P(), P(), P())
    return jax.shard_map(local, mesh=mesh, in_specs=in_specs, out_specs=out_specs, check_vma=False)
```

profile of v0, /device:TPU:0, one launch (start us, length us, event | category | flops | bytes accessed | tf_op | source)
XLA Modules:
  0.0 43.9 jit_solution(1927783430298262876)
XLA Ops:
  0.6 0.0 copy-start.6
  0.6 0.7 %multiply_bitcast_fusion = s32[2,8]{1,0:T(2,128)S(1)} fusion(s32[8,2]{0,1:T(2,128)} %param.9, s32[]{:T(128)S(6)} %mul.10), kind=kLoop, calls=%fused_computation.10 | loop fusion | flops 32 | bytes 132 | tf_op jit(solution)/shard_map/mul | solution.py:399
  1.3 0.1 add.31
  1.4 0.0 copy-done.6
  1.4 0.0 copy-start.5
  1.5 0.1 fusion.1.pick_ref
  1.6 0.8 %copy-done.5 = bf16[2,12,6,256]{3,0,2,1:T(2,128)(2,1)S(1)} copy-done((bf16[2,12,6,256]{3,0,2,1:T(2,128)(2,1)S(1)}, bf16[2,12,6,256]{3,0,2,1:T(2,128)(2,1)}, u32[]{:S(2)}) %copy-start.5) | copy-done | bytes 73752
  2.3 0.0 copy-start
  2.3 0.1 reshape.77
  2.4 0.0 copy-start.1
  2.4 0.0 copy-start.2
  2.5 0.0 copy-start.3
  2.5 0.0 copy-start.4
  2.5 0.1 fusion.avg_ref
  2.6 0.7 %copy-done = bf16[2,3,3,64,64]{4,3,2,1,0:T(8,128)(2,1)S(1)} copy-done((bf16[2,3,3,64,64]{4,3,2,1,0:T(8,128)(2,1)S(1)}, bf16[2,3,3,64,64]{4,3,2,1,0:T(8,128)(2,1)}, u32[]{:S(2)}) %copy-start) | copy-done | bytes 147480
  3.3 0.0 copy-done.1
  3.3 0.0 copy-done.2
  3.3 0.0 copy-done.3
  3.3 0.0 copy-done.4
  3.3 39.5 %shard_map.127 = (f32[4,16,128]{2,1,0:T(8,128)S(1)}, f32[640,128]{1,0:T(8,128)S(1)}, f32[24,128]{1,0:T(8,128)S(1)}) custom-call(bf16[48,768]{1,0:T(8,128)(2,1)S(1)} %bitcast.19, bf16[64,144]{1,0:T(8,128)(2,1)S(1)} %fusion.1.pick_ref, f32[256,128]{1,0:T(8,128)S(1)} %fusion.avg_ref, f32[4,16,128]{2,1,0:T(8,128)S(1)} %pad.4.tgt_ref, ...), custom_call_target="tpu_custom_call" | custom-call | tf_op jit(solution)/shard_map/pallas_call | solution.py:413
  42.8 1.0 %shard_map.128 = (f32[2,3,8,64]{3,2,1,0:T(8,128)}, f32[3,3,2,64]{3,2,1,0:T(2,128)}, f32[2,64]{1,0:T(2,128)}, f32[2,3,3,64,64]{4,3,2,1,0:T(8,128)}, f32[2,64]{1,0:T(2,128)}, /*index=5*/f32[3,3,2,64]{3,2,1,0:T(2,128)}) custom-call(f32[4,16,128]{2,1,0:T(8,128)S(1)} %get-tuple-element.15.den, f32[640,128]{1,0:T(8,128)S(1)} %get-tuple-element.16.sums, ...), custom_call_target="tpu_custom_call" | custom-call | tf_op jit(solution)/shard_map/pallas_call | solution.py:472
  (7 shorter events, 0.1 us)
Async XLA Ops:
  0.6 0.8 %copy-start.6 = (f32[2,8,3,64]{3,1,2,0:T(8,128)S(1)}, f32[2,8,3,64]{3,1,2,0:T(8,128)}, u32[]{:S(2)}) copy-start(f32[2,8,3,64]{3,1,2,0:T(8,128)} %param.10) | copy-start | bytes 36868
  1.4 0.9 %copy-start.5 = (bf16[2,12,6,256]{3,0,2,1:T(2,128)(2,1)S(1)}, bf16[2,12,6,256]{3,0,2,1:T(2,128)(2,1)}, u32[]{:S(2)}) copy-start(bf16[2,12,6,256]{3,0,2,1:T(2,128)(2,1)} %param.8) | copy-start | bytes 221188
  2.3 1.0 %copy-start = (bf16[2,3,3,64,64]{4,3,2,1,0:T(8,128)(2,1)S(1)}, bf16[2,3,3,64,64]{4,3,2,1,0:T(8,128)(2,1)}, u32[]{:S(2)}) copy-start(bf16[2,3,3,64,64]{4,3,2,1,0:T(8,128)(2,1)} %wmid_any.1) | copy-start | bytes 442372
  2.4 0.9 %copy-start.1 = (bf16[2,3,3,64]{3,0,2,1:T(2,128)(2,1)S(1)}, bf16[2,3,3,64]{3,0,2,1:T(2,128)(2,1)}, u32[]{:S(2)}) copy-start(bf16[2,3,3,64]{3,0,2,1:T(2,128)(2,1)} %param.11) | copy-start | bytes 6916
  2.4 0.8 %copy-start.2 = (bf16[2,3,3,64]{3,0,2,1:T(2,128)(2,1)S(1)}, bf16[2,3,3,64]{3,0,2,1:T(2,128)(2,1)}, u32[]{:S(2)}) copy-start(bf16[2,3,3,64]{3,0,2,1:T(2,128)(2,1)} %param.15) | copy-start | bytes 6916
  2.5 0.8 %copy-start.3 = (bf16[2,64]{1,0:T(2,128)(2,1)S(1)}, bf16[2,64]{1,0:T(2,128)(2,1)}, u32[]{:S(2)}) copy-start(bf16[2,64]{1,0:T(2,128)(2,1)} %bl_any.1) | copy-start | bytes 772
  2.5 0.8 %copy-start.4 = (bf16[2,64]{1,0:T(2,128)(2,1)S(1)}, bf16[2,64]{1,0:T(2,128)(2,1)}, u32[]{:S(2)}) copy-start(bf16[2,64]{1,0:T(2,128)(2,1)} %bmid_any.1) | copy-start | bytes 772
where the time goes:
time: 44.7 us; the launch traced here: 43.9 us
  Pallas kernels  40.5 us (91%)
  local copies, waits for them, and re-layouts  1.69 us (4%)
  other arithmetic  0.87 us (2%)
  between operations  0.76 us (2%)
    pallas_call x1, Pallas kernels, local(): pl.pallas_call(functools.partial(step_kernel, (n_row, n_col, n_date, pp,...  39.5 us
    unnamed x15, local copies, waits for them, and re-layouts  1.51 us
    pallas_call x1, Pallas kernels, local(): pl.pallas_call(functools.partial(finish_kernel, (n_row, pp, tr, tc, ch)),...  1.05 us

commit v1 on v0

--- a/solution.py
+++ b/solution.py
@@ -364,6 +364,10 @@
             for t in range(tr):
                 at = (z * tr + t) * pp
                 den_out[z, t, k * pp : (k + 1) * pp, :] = den[k, at : at + pp, 0:tc]
+    finish_grads(ch, sums, small, lift_out, lbias_out, mid_out, mbias_out, proj_out)
+
+
+def finish_grads(ch, sums, small, lift_out, lbias_out, mid_out, mbias_out, proj_out):
     for t in range(3):
         for u in range(3):
             at = 8 * t + 2 * u
@@ -382,7 +386,7 @@
         mbias_out[z : z + 1, :] = sums[600:601, z * ch : (z + 1) * ch]
 
 
-def local(slc, pairs, target, w_lift, b_lift, w_mid, b_mid, w_proj):
+def halo_local(slc, pairs, target, w_lift, b_lift, w_mid, b_mid, w_proj):
     n_row, n_col, n_date = (lax.axis_size(axis) for axis in ("row", "col", "date"))
     dates, srows, scols = slc.shape[1:]
     count, tr, tc = target.shape[1:]
@@ -493,6 +497,488 @@
     )
 
 
+def whole_kernel(
+    dims, scale,
+    slc_ref, idx_any, tgt_any, wl_any, bl_any, wmid_any, bmid_any, wproj_any,
+    den_ref, o_ref, small_ref,
+    pool, idx_in, tgt_in, look_s, look_r, tgt_s, tgt_r, fld, tfld, i3a, i3b, h2s, tsum, dn3, dp1, outs, x_ref,
+    wl_in, bl_in, wm_in, bm_in, wj_in, w_sem, w1_ref, wp_ref, wpb_ref, wf_ref, wb_ref, bm_ref, wtmp,
+    plane_in, date_in, small_in, small_date, small_sem, small_date_sem, slab_sem, look_sem, tgt_sem, den_sem, plane_sem, date_sem, gather_sem,
+):
+    n_row, n_col, n_date, dates, tr, tc = dims
+    r, c, d = lax.axis_index("row"), lax.axis_index("col"), lax.axis_index("date")
+    n_plane = n_row * n_col
+    me = r * n_col + c
+    pairs = n_plane
+    nb = n_row * tr
+    n = nb * 128
+    wide = n + 256
+    f32, bf16 = jnp.float32, jnp.bfloat16
+
+    def plane_peer(k):
+        peer = lax.rem(me + k, n_plane)
+        return peer, (lax.div(peer, n_col), lax.rem(peer, n_col), d)
+
+    def date_peer(k):
+        return (r, c, lax.rem(d + k, n_date))
+
+    def remote_of(src, dst, sems, at, where):
+        return pltpu.make_async_remote_copy(
+            src_ref=src, dst_ref=dst, send_sem=sems.at[0, at], recv_sem=sems.at[1, at],
+            device_id=where, device_id_type=MESH,
+        )
+
+    def remote(src, dst, sems, at, where):
+        copy = remote_of(src, dst, sems, at, where)
+        copy.start()
+        return copy
+
+    barrier = pltpu.get_barrier_semaphore()
+    for k in range(1, n_date):
+        pl.semaphore_signal(barrier, inc=1, device_id=date_peer(k), device_id_type=MESH)
+    for k in range(1, n_plane):
+        pl.semaphore_signal(barrier, inc=1, device_id=plane_peer(k)[1], device_id_type=MESH)
+    fetches = []
+    wide_in = zip(
+        (idx_any, tgt_any, wl_any, bl_any, wmid_any, bmid_any, wproj_any),
+        (idx_in, tgt_in, wl_in, bl_in, wm_in, bm_in, wj_in),
+    )
+    for k, (src, dst) in enumerate(wide_in):
+        copy = pltpu.make_async_copy(src, dst, w_sem.at[k])
+        copy.start()
+        fetches.append(copy)
+    pl.semaphore_wait(barrier, n_plane + n_date - 2)
+
+    slab = slc_ref.shape[0]
+    chunk = LR * 128
+    down = lax.max(d - 1, 0)
+
+    def own_slab(t):
+        lanes = pl.ds(t * chunk, chunk)
+        return remote_of(slc_ref.at[:, lanes], pool.at[pl.ds(slab, slab), lanes], slab_sem, t, (r, c, down))
+
+    def far_slab(t):
+        lanes = pl.ds(t * chunk, chunk)
+        return remote_of(
+            pool.at[pl.ds(slab, slab), lanes], pool.at[pl.ds(2 * slab, slab), lanes], slab_sem, tr + t, (r, c, down)
+        )
+
+    has_down = d > 0
+    has_one = d < n_date - 1
+    has_two = d < n_date - 2
+
+    @pl.when(has_down)
+    def _():
+        for t in range(tr):
+            own_slab(t).start()
+
+    @pl.when(jnp.logical_not(has_one))
+    def _():
+        pool[slab : 2 * slab, :] = jnp.zeros((slab, tr * chunk), bf16)
+
+    @pl.when(jnp.logical_not(has_two))
+    def _():
+        pool[2 * slab : 3 * slab, :] = jnp.zeros((slab, tr * chunk), bf16)
+
+    pool[0:slab, :] = slc_ref[...]
+    for ref in (fld, tfld, dn3, tsum, tgt_s, look_s):
+        ref[...] = jnp.zeros_like(ref)
+    edge = jnp.zeros((i3a.shape[0], 128), bf16)
+    for ref in (i3a, i3b):
+        ref[:, 0:128] = edge
+        ref[:, (nb + 1) * 128 : (nb + 2) * 128] = edge
+    x_ref[608:, :] = jnp.zeros((x_ref.shape[0] - 608, 128), f32)
+    outs[...] = jnp.zeros_like(outs)
+    lane = lax.broadcasted_iota(jnp.int32, (1, 128), 1)
+    for copy in fetches[:2]:
+        copy.wait()
+
+    def to_lane(value):
+        return pltpu.roll(jnp.concatenate([value, jnp.zeros((value.shape[0], 128 - tc), f32)], axis=1), c * tc, 1)
+
+    for z in range(2):
+        for t in range(tr):
+            block = to_lane(tgt_in[z, t])
+            for k in range(pairs):
+                tgt_s[k, z * tr + t : z * tr + t + 1, :] = block[k : k + 1]
+
+    def exchange(src, dst, sems):
+        dst[me] = src[me]
+        return [remote(src.at[plane_peer(k)[0]], dst.at[me], sems, k, plane_peer(k)[1]) for k in range(1, n_plane)]
+
+    halves = tc * LC // 128
+    kinds = 2 * halves
+    index = idx_in[...] - d * dates
+    spread_lanes = jnp.concatenate([index[0:1]] * kinds + [index[1:2]] * kinds, axis=1)
+    row_of = lax.broadcasted_iota(jnp.int32, (slab, 2 * kinds * pairs), 0)
+    lane_of = lax.broadcasted_iota(jnp.int32, (slab, 2 * kinds * pairs), 1)
+    same_kind = lax.rem(row_of, kinds) == lax.rem(lax.div(lane_of, pairs), kinds)
+    picks = []
+    for s in range(3):
+        hit = same_kind & (lax.div(row_of, kinds) + s * dates == spread_lanes)
+        picks.append(jnp.where(hit, 1.0, 0.0).astype(f32))
+    pick = jnp.concatenate(picks, axis=0).T.astype(bf16)
+    spots = lax.broadcasted_iota(jnp.int32, (tc * LC, 128), 0)
+    avg_lane = lax.broadcasted_iota(jnp.int32, (tc * LC, 128), 1)
+    avg = jnp.where(lax.div(spots, LC) + c * tc == avg_lane, 1.0 / (LR * LC), 0.0).astype(f32)
+
+    @pl.when(has_one)
+    def _():
+        for t in range(tr):
+            own_slab(t).wait_recv()
+
+            @pl.when(has_down)
+            def _():
+                far_slab(t).start()
+
+    tgt_copies = exchange(tgt_s, tgt_r, tgt_sem)
+
+    for copy in fetches[2:]:
+        copy.wait()
+    wtmp[...] = jnp.zeros_like(wtmp)
+
+    def joined(a, b):
+        return jnp.concatenate([a, b], axis=1)
+
+    for t in range(3):
+        for u in range(3):
+            pair = wl_in[t, u].astype(f32)
+            at = 8 * t + 2 * u
+            wtmp[0, at : at + 1, :] = joined(pair[0:1], pair[1:2])
+            wtmp[0, at + 1 : at + 2, :] = joined(-pair[1:2], pair[0:1])
+            pair = wj_in[t, u].astype(f32)
+            real, imag = joined(pair[0:1], -pair[1:2]), joined(pair[1:2], pair[0:1])
+            flip = 8 * (2 - t) + 2 * (2 - u)
+            wtmp[1, at : at + 1, :] = real
+            wtmp[1, at + 1 : at + 2, :] = imag
+            wtmp[2, flip : flip + 1, :] = real
+            wtmp[2, flip + 1 : flip + 2, :] = imag
+            wr, wi = wm_in[0, t, u].astype(f32), wm_in[1, t, u].astype(f32)
+            block = jnp.concatenate([joined(wr, wi), joined(-wi, wr)], axis=0)
+            wb_ref[2 - t, :, (2 - u) * 128 : (3 - u) * 128] = block.astype(bf16)
+            wf_ref[t, :, u * 128 : (u + 1) * 128] = block.T.astype(bf16)
+    bias = bl_in[...].astype(f32)
+    wtmp[0, 14:15, :] = joined(bias[0:1], bias[1:2])
+    bias = bm_in[...].astype(f32)
+    wtmp[3, 0:1, :] = joined(bias[0:1], bias[1:2])
+    w1_ref[...] = wtmp[0].T[:, 0:32].astype(bf16)
+    wp_ref[...] = wtmp[1, 0:32].astype(bf16)
+    wpb_ref[...] = wtmp[2].T[:, 0:32].astype(bf16)
+    bm_ref[...] = wtmp[3].T[:, 0:1]
+    fld[6:7, :] = jnp.ones((1, wide), f32)
+
+    def rounded(value):
+        return value.astype(bf16).astype(f32)
+
+    for t in range(tr):
+
+        @pl.when(has_two)
+        def _():
+            far_slab(t).wait_recv()
+
+        picked = mm(pick, pool[:, t * chunk : (t + 1) * chunk])
+        sides = []
+        for h in range(halves):
+            a0, a1, b0, b1 = [picked[q * pairs : (q + 1) * pairs] for q in (h, halves + h, 2 * halves + h, 3 * halves + h)]
+            both = []
+            for prod in (a0 * b0 + a1 * b1, a1 * b0 - a0 * b1):
+                both.append(sum(prod[:, q * 128 : (q + 1) * 128] for q in range(LR)))
+            sides.append(jnp.concatenate(both, axis=0))
+        looked = rounded(
+            jnp.dot(
+                jnp.concatenate(sides, axis=1), avg,
+                precision=lax.Precision.HIGHEST, preferred_element_type=f32,
+            )
+        )
+        for z in range(2):
+            for k in range(pairs):
+                at = z * tr + t
+                look_s[k, at : at + 1, :] = looked[z * pairs + k : z * pairs + k + 1]
+    look_copies = exchange(look_s, look_r, look_sem)
+
+    def settle(copies):
+        for copy in copies:
+            copy.wait_recv()
+
+    first, last = lane == 0, lane == 127
+
+    def right(value):
+        return jnp.where(first, 0.0, pltpu.roll(value, 1, 1))
+
+    def left(value):
+        return jnp.where(last, 0.0, pltpu.roll(value, 127, 1))
+
+    def assemble(ref, s):
+        return functools.reduce(lambda a, b: a + b, [ref[s * n_col + q] for q in range(n_col)])
+
+    settle(tgt_copies)
+    for s in range(n_row):
+        block = assemble(tgt_r, s)
+        for z in range(2):
+            for t in range(tr):
+                b = s * tr + t
+                tfld[z : z + 1, b * 128 : (b + 1) * 128] = block[z * tr + t : z * tr + t + 1]
+    settle(look_copies)
+    for s in range(n_row):
+        block = assemble(look_r, s)
+        for u, turned in enumerate((right(block), block, left(block))):
+            for z in range(2):
+                for t in range(tr):
+                    b = s * tr + t + 1
+                    fld[2 * u + z : 2 * u + z + 1, b * 128 : (b + 1) * 128] = turned[z * tr + t : z * tr + t + 1]
+
+    def taps(ref, at, width):
+        three = [ref[:, at + t * 128 : at + t * 128 + width] for t in range(3)]
+        return jnp.concatenate(three + [jnp.zeros((8, width), f32)], axis=0).astype(bf16)
+
+    def turned_store(ref, value, at):
+        for q in range(2):
+            piece = value[:, q * 128 : (q + 1) * 128]
+            lanes = slice(at + (q + 1) * 128, at + (q + 2) * 128)
+            for u, turned in enumerate((right(piece), piece, left(piece))):
+                ref[u * 128 : (u + 1) * 128, lanes] = turned.astype(bf16)
+
+    for at in range(0, n, 256):
+        pre1 = mm(w1_ref[...], taps(fld, at, 256))
+        turned_store(i3a, rounded(jnp.maximum(pre1, 0.0)), at)
+
+    def conv(w_ref, ref, at):
+        total = 0.0
+        for t in range(3):
+            total = total + mm(w_ref[t], ref[:, at + t * 128 : at + t * 128 + 256])
+        return total
+
+    for at in range(0, n, 256):
+        pre2 = conv(wf_ref, i3a, at) + bm_ref[...]
+        h2 = jnp.maximum(pre2, 0.0).astype(bf16)
+        h2s[:, at : at + 256] = h2
+        tsum[:, at + 128 : at + 384] = mm(wp_ref[...], h2)
+
+    wide_lane = lax.rem(lax.broadcasted_iota(jnp.int32, (1, n), 1), 128)
+    wide_first, wide_last = wide_lane == 0, wide_lane == 127
+
+    def wide_right(value):
+        return jnp.where(wide_first, 0.0, pltpu.roll(value, 1, 1))
+
+    def wide_left(value):
+        return jnp.where(wide_last, 0.0, pltpu.roll(value, n - 1, 1))
+
+    six = sum(tsum[8 * t : 8 * t + 8, t * 128 : t * 128 + n] for t in range(3))
+    noise = wide_right(six)[0:2] + six[2:4] + wide_left(six)[4:6]
+    den = fld[2:4, 128 : 128 + n] - noise
+    for q in range(n_col):
+        shifted = pltpu.roll(den, n - q * tc, 1) if q else den
+        for s in range(n_row):
+            for z in range(2):
+                for t in range(tr):
+                    i, b = z * tr + t, s * tr + t
+                    outs[s * n_col + q, i : i + 1, :] = shifted[z : z + 1, b * 128 : (b + 1) * 128]
+    den_copies = exchange(outs, den_ref, den_sem)
+    dn = rounded((tfld[0:2, :] - den) * scale)
+    dn3[0:2, 128 : 128 + n] = wide_right(dn)
+    dn3[2:4, 128 : 128 + n] = dn
+    dn3[4:6, 128 : 128 + n] = wide_left(dn)
+
+    for at in range(0, n, 256):
+        grad = mm(wpb_ref[...], taps(dn3, at, 256))
+        grad = rounded(jnp.where(h2s[:, at : at + 256].astype(f32) > 0, grad, 0.0))
+        turned_store(i3b, grad, at)
+
+    sign = jnp.where(lane < 64, 1.0, -1.0)
+    dp2 = i3b[128:256, 128 : 128 + n]
+    for t in range(3):
+        gram = mm_t(i3a[:, t * 128 : t * 128 + n], dp2)
+        for u in range(3):
+            upper = gram[u * 128 : u * 128 + 64]
+            lower = gram[u * 128 + 64 : u * 128 + 128]
+            x_ref[(3 * t + u) * 64 : (3 * t + u) * 64 + 64, :] = upper + sign * pltpu.roll(lower, 64, 1)
+    x_ref[576:600, :] = mm_t(taps(dn3, 0, n), h2s[...])[0:24]
+    x_ref[600:608, :] = mm_t(jnp.ones((16, n), bf16), dp2)[0:8]
+
+    piece = plane_in.shape[1]
+
+    def slot(ref, k):
+        return ref.at[pl.ds(pl.multiple_of(k * piece, 8), piece)]
+
+    scatter = []
+    for k in range(1, n_plane):
+        peer, where = plane_peer(k)
+        scatter.append(remote(slot(x_ref, peer), plane_in.at[k], plane_sem, k, where))
+
+    for at in range(0, n, 256):
+        h1 = i3a[128:256, at + 128 : at + 384].astype(f32)
+        grad = jnp.where(h1 > 0, conv(wb_ref, i3b, at), 0.0)
+        dp1[:, at : at + 256] = grad.astype(bf16)
+
+    small_in[me] = mm_t(taps(fld, 0, n), dp1[...])[0:24]
+    small = [
+        remote(small_in.at[me], small_in.at[me], small_sem, k, plane_peer(k)[1]) for k in range(1, n_plane)
+    ]
+    part = slot(x_ref, me)[...]
+    for k, copy in zip(range(1, n_plane), scatter):
+        copy.wait_recv()
+        part = part + plane_in[k]
+    date_in[d] = part
+    spread = [remote(date_in.at[d], date_in.at[d], date_sem, k, date_peer(k)) for k in range(1, n_date)]
+
+    def total(ref, count):
+        return functools.reduce(lambda a, b: a + b, [ref[k] for k in range(count)])
+
+    settle(small)
+    small_date[d] = total(small_in, n_plane)
+    small_spread = [
+        remote(small_date.at[d], small_date.at[d], small_date_sem, k, date_peer(k)) for k in range(1, n_date)
+    ]
+    settle(spread)
+    slot(o_ref, me)[...] = total(date_in, n_date)
+    gather = [
+        remote(slot(o_ref, me), slot(o_ref, me), gather_sem, k, plane_peer(k)[1])
+        for k in range(1, n_plane)
+    ]
+    settle(small_spread)
+    small_ref[...] = total(small_date, n_date)
+    settle(den_copies)
+    settle(gather)
+
+    @pl.when(has_down)
+    def _():
+        for t in range(tr):
+            own_slab(t).wait_send()
+
+    @pl.when(has_down & has_one)
+    def _():
+        for t in range(tr):
+            far_slab(t).wait_send()
+
+    for copy in tgt_copies + look_copies + den_copies + scatter + small + spread + small_spread + gather:
+        copy.wait_send()
+
+
+def whole_finish(dims, den, sums, small, den_out, lift_out, lbias_out, mid_out, mbias_out, proj_out):
+    n_plane, tr, tc, ch = dims
+    for z in range(2):
+        for t in range(tr):
+            for k in range(n_plane):
+                den_out[z, t, k : k + 1, :] = den[k, z * tr + t : z * tr + t + 1, 0:tc]
+    finish_grads(ch, sums, small, lift_out, lbias_out, mid_out, mbias_out, proj_out)
+
+
+def whole_local(slc, pairs, target, w_lift, b_lift, w_mid, b_mid, w_proj):
+    n_row, n_col, n_date = (lax.axis_size(axis) for axis in ("row", "col", "date"))
+    dates, srows, scols = slc.shape[1:]
+    count, tr, tc = target.shape[1:]
+    ch = w_mid.shape[-1]
+    halves = scols // 128
+    bf16, f32 = jnp.bfloat16, jnp.float32
+    packed = slc.reshape(2, dates, srows, halves, 128).transpose(1, 0, 3, 2, 4)
+    packed = packed.reshape(dates * 2 * halves, srows * 128)
+    tgt = target.transpose(0, 2, 1, 3)
+    w_lift, w_proj = w_lift.transpose(1, 2, 0, 3), w_proj.transpose(1, 2, 0, 3)
+    scale = 1.0 / math.sqrt(2.0 * count * n_date * tr * n_row * tc * n_col)
+    nb = n_row * tr
+    n, wide = nb * 128, (nb + 2) * 128
+    n_plane = n_row * n_col
+    piece = -(-608 // (8 * n_plane)) * 8
+    zt = -(-2 * tr // 8) * 8
+    dma = pltpu.SemaphoreType.DMA
+    vmem = pltpu.VMEM
+    shape = jax.ShapeDtypeStruct
+    den, sums, small = pl.pallas_call(
+        functools.partial(whole_kernel, (n_row, n_col, n_date, dates, tr, tc), scale),
+        out_shape=(
+            shape((n_plane, zt, 128), f32),
+            shape((n_plane * piece, 128), f32),
+            shape((24, 128), f32),
+        ),
+        in_specs=[pl.BlockSpec(memory_space=vmem)] + [pl.BlockSpec(memory_space=pltpu.HBM)] * 7,
+        out_specs=(pl.BlockSpec(memory_space=vmem),) * 3,
+        scratch_shapes=[
+            vmem((3 * packed.shape[0], packed.shape[1]), bf16),
+            vmem((2, count), jnp.int32),
+            vmem(tgt.shape, f32),
+            vmem((n_plane, zt, 128), f32),
+            vmem((n_plane, zt, 128), f32),
+            vmem((n_plane, zt, 128), f32),
+            vmem((n_plane, zt, 128), f32),
+            vmem((8, wide), f32),
+            vmem((8, n), f32),
+            vmem((6 * ch, wide), bf16),
+            vmem((6 * ch, wide), bf16),
+            vmem((2 * ch, n), bf16),
+            vmem((32, wide), f32),
+            vmem((8, wide), f32),
+            vmem((2 * ch, n), bf16),
+            vmem((n_plane, zt, 128), f32),
+            vmem((n_plane * piece, 128), f32),
+            vmem(w_lift.shape, bf16),
+            vmem(b_lift.shape, bf16),
+            vmem(w_mid.shape, bf16),
+            vmem(b_mid.shape, bf16),
+            vmem(w_proj.shape, bf16),
+            dma((7,)),
+            vmem((2 * ch, 32), bf16),
+            vmem((32, 2 * ch), bf16),
+            vmem((2 * ch, 32), bf16),
+            vmem((3, 2 * ch, 6 * ch), bf16),
+            vmem((3, 2 * ch, 6 * ch), bf16),
+            vmem((2 * ch, 1), f32),
+            vmem((4, 128, 128), f32),
+            vmem((n_plane, piece, 128), f32),
+            vmem((n_date, piece, 128), f32),
+            vmem((n_plane, 24, 128), f32),
+            vmem((n_date, 24, 128), f32),
+            dma((2, n_plane)),
+            dma((2, n_date)),
+            dma((2, 2 * tr)),
+            dma((2, n_plane)),
+            dma((2, n_plane)),
+            dma((2, n_plane)),
+            dma((2, n_plane)),
+            dma((2, n_date)),
+            dma((2, n_plane)),
+        ],
+        compiler_params=pltpu.CompilerParams(
+            collective_id=0, has_side_effects=True, vmem_limit_bytes=48 * 1024 * 1024
+        ),
+    )(packed, pairs.T, tgt, w_lift, b_lift, w_mid, b_mid, w_proj)
+    denoised, grad_lift, lift_bias, grad_mid, mid_bias, grad_proj = pl.pallas_call(
+        functools.partial(whole_finish, (n_plane, tr, tc, ch)),
+        out_shape=(
+            shape((2, tr, count, tc), f32),
+            shape((3, 3, 2, ch), f32),
+            shape((2, ch), f32),
+            shape((2, 3, 3, ch, ch), f32),
+            shape((2, ch), f32),
+            shape((3, 3, 2, ch), f32),
+        ),
+        in_specs=[pl.BlockSpec(memory_space=vmem)] * 3,
+        out_specs=(pl.BlockSpec(memory_space=vmem),) * 6,
+        compiler_params=pltpu.CompilerParams(vmem_limit_bytes=8 * 1024 * 1024),
+    )(den, sums, small)
+    return (
+        denoised.transpose(0, 2, 1, 3),
+        grad_lift.transpose(2, 0, 1, 3),
+        lift_bias,
+        grad_mid,
+        mid_bias,
+        grad_proj.transpose(2, 0, 1, 3),
+    )
+
+
+def local(slc, pairs, target, *weights):
+    n_row, n_col = lax.axis_size("row"), lax.axis_size("col")
+    count, tr, tc = target.shape[1:]
+    whole = (
+        count == n_row * n_col
+        and tc * n_col == 128
+        and (n_row * tr) % 2 == 0
+        and 2 * tr <= 8
+        and count == 8
+        and (2 * slc.shape[1] * slc.shape[3] // 128) % 16 == 0
+    )
+    return (whole_local if whole else halo_local)(slc, pairs, target, *weights)
+
+
 def solution(mesh):
     in_specs = (
         P(None, "date", "row", "col"),

time: 44.7 us -> 38.9 us (0.87)
  Pallas kernels: 40.5 us -> 36 us
  other arithmetic: 0.87 us -> 0 us
    pallas_call x2, Pallas kernels: 40.5 us -> 36 us  [the longest x1 35 us: whole_local(): pl.pallas_call(functools.partial(whole_kernel, (n_row, n_col, n_date, dat...]
    reshape x4 -> x2, local copies, waits for them, and re-layouts: 0.08 us -> 1 us  [whole_local(): packed = slc.reshape(2, dates, srows, halves, 128).transpose(1, 0, 3, 2, 4)]
    unnamed x15, local copies, waits for them, and re-layouts: 1.51 us -> 0.69 us
    mul x1 -> x0, other arithmetic: 0.68 us -> none  [local(): index[:, None, :] * kinds]
where the time goes in v1:
time: 38.9 us; the launch traced here: 38.5 us
  Pallas kernels  36 us (93%)
  local copies, waits for them, and re-layouts  1.69 us (4%)
  between operations  0.73 us (2%)
    pallas_call x1, Pallas kernels, whole_local(): pl.pallas_call(functools.partial(whole_kernel, (n_row, n_col, n_date, dat...  35 us
    pallas_call x1, Pallas kernels, whole_local(): pl.pallas_call(functools.partial(whole_finish, (n_plane, tr, tc, ch)), ou...  1.05 us
    reshape x2, local copies, waits for them, and re-layouts, whole_local(): packed = slc.reshape(2, dates, srows, halves, 128).transpose(1, 0, 3, 2, 4)  1 us

profile of v1, /device:TPU:0, one launch (start us, length us, event | category | flops | bytes accessed | tf_op | source)
XLA Modules:
  0.0 38.5 jit_solution(7196841957191693209)
XLA Ops:
  0.6 0.0 copy-start
  0.6 1.0 %reshape.18 = bf16[2,12,6,2,128]{4,3,0,2,1:T(2,128)(2,1)S(1)} reshape(bf16[2,12,6,256]{3,0,2,1:T(2,128)(2,1)} %param.8) | data formatting | bytes 147456 | tf_op jit(solution)/shard_map/reshape | solution.py:873
  1.7 0.0 copy-start.1
  1.7 0.0 copy-start.2
  1.7 0.0 copy-start.3
  1.7 0.0 copy-start.6
  1.7 0.0 copy-start.4
  1.7 0.0 copy-start.5
  1.7 0.0 copy-done
  1.8 0.6 %copy-done.1 = f32[2,8,3,64]{3,1,2,0:T(8,128)S(1)} copy-done((f32[2,8,3,64]{3,1,2,0:T(8,128)S(1)}, f32[2,8,3,64]{3,1,2,0:T(8,128)}, u32[]{:S(2)}) %copy-start.1) | copy-done | bytes 12312
  2.4 0.0 copy-done.2
  2.4 0.0 copy-done.3
  2.4 0.0 copy-done.6
  2.4 0.0 copy-done.4
  2.4 0.0 copy-done.5
  2.4 35.0 %shard_map.127 = (f32[8,8,128]{2,1,0:T(8,128)S(1)}, f32[640,128]{1,0:T(8,128)S(1)}, f32[24,128]{1,0:T(8,128)S(1)}) custom-call(bf16[48,768]{1,0:T(8,128)(2,1)S(1)} %bitcast.15, s32[2,8]{1,0:T(2,128)S(1)} %bitcast.19, f32[2,3,8,64]{3,2,1,0:T(8,128)S(1)} %bitcast.16, bf16[3,3,2,64]{3,2,1,0:T(2,128)(2,1)S(1)} %bitcast.17, bf16[2,64]{1,0:T(2,128)(2,1)S(1)} %copy-done.5, ...), custom_call_target="tpu_custom_call" | custom-call | tf_op jit(solution)/shard_map/pallas_call | solution.py:886
  37.4 1.0 %shard_map.128 = (f32[2,3,8,64]{3,2,1,0:T(8,128)}, f32[3,3,2,64]{3,2,1,0:T(2,128)}, f32[2,64]{1,0:T(2,128)}, f32[2,3,3,64,64]{4,3,2,1,0:T(8,128)}, f32[2,64]{1,0:T(2,128)}, /*index=5*/f32[3,3,2,64]{3,2,1,0:T(2,128)}) custom-call(f32[8,8,128]{2,1,0:T(8,128)S(1)} %get-tuple-element.15.den, f32[640,128]{1,0:T(8,128)S(1)} %get-tuple-element.16.sums, ...), custom_call_target="tpu_custom_call" | custom-call | tf_op jit(solution)/shard_map/pallas_call | solution.py:944
  (2 shorter events, 0.0 us)
Async XLA Ops:
  0.6 1.1 %copy-start = (bf16[2,3,3,64,64]{4,3,2,1,0:T(8,128)(2,1)S(1)}, bf16[2,3,3,64,64]{4,3,2,1,0:T(8,128)(2,1)}, u32[]{:S(2)}) copy-start(bf16[2,3,3,64,64]{4,3,2,1,0:T(8,128)(2,1)} %wmid_any.1) | copy-start | bytes 442372
  1.7 0.7 %copy-start.1 = (f32[2,8,3,64]{3,1,2,0:T(8,128)S(1)}, f32[2,8,3,64]{3,1,2,0:T(8,128)}, u32[]{:S(2)}) copy-start(f32[2,8,3,64]{3,1,2,0:T(8,128)} %param.10) | copy-start | bytes 36868
  1.7 0.7 %copy-start.2 = (bf16[2,3,3,64]{3,0,2,1:T(2,128)(2,1)S(1)}, bf16[2,3,3,64]{3,0,2,1:T(2,128)(2,1)}, u32[]{:S(2)}) copy-start(bf16[2,3,3,64]{3,0,2,1:T(2,128)(2,1)} %param.11) | copy-start | bytes 6916
  1.7 0.7 %copy-start.3 = (bf16[2,3,3,64]{3,0,2,1:T(2,128)(2,1)S(1)}, bf16[2,3,3,64]{3,0,2,1:T(2,128)(2,1)}, u32[]{:S(2)}) copy-start(bf16[2,3,3,64]{3,0,2,1:T(2,128)(2,1)} %param.15) | copy-start | bytes 6916
  1.7 0.7 %copy-start.6 = (bf16[2,64]{1,0:T(2,128)(2,1)S(1)}, bf16[2,64]{1,0:T(2,128)(2,1)}, u32[]{:S(2)}) copy-start(bf16[2,64]{1,0:T(2,128)(2,1)} %bmid_any.1) | copy-start | bytes 772
  1.7 0.7 %copy-start.4 = (s32[8,2]{0,1:T(2,128)S(1)}, s32[8,2]{0,1:T(2,128)}, u32[]{:S(2)}) copy-start(s32[8,2]{0,1:T(2,128)} %param.9) | copy-start | bytes 196
  1.7 0.7 %copy-start.5 = (bf16[2,64]{1,0:T(2,128)(2,1)S(1)}, bf16[2,64]{1,0:T(2,128)(2,1)}, u32[]{:S(2)}) copy-start(bf16[2,64]{1,0:T(2,128)(2,1)} %bl_any.1) | copy-start | bytes 772

commit v2 on v1

--- a/solution.py
+++ b/solution.py
@@ -500,10 +500,10 @@
 def whole_kernel(
     dims, scale,
     slc_ref, idx_any, tgt_any, wl_any, bl_any, wmid_any, bmid_any, wproj_any,
-    den_ref, o_ref, small_ref,
+    den_ref, o_ref,
     pool, idx_in, tgt_in, look_s, look_r, tgt_s, tgt_r, fld, tfld, i3a, i3b, h2s, tsum, dn3, dp1, outs, x_ref,
     wl_in, bl_in, wm_in, bm_in, wj_in, w_sem, w1_ref, wp_ref, wpb_ref, wf_ref, wb_ref, bm_ref, wtmp,
-    plane_in, date_in, small_in, small_date, small_sem, small_date_sem, slab_sem, look_sem, tgt_sem, den_sem, plane_sem, date_sem, gather_sem,
+    plane_in, date_in, slab_sem, look_sem, tgt_sem, den_sem, sum_sem,
 ):
     n_row, n_col, n_date, dates, tr, tc = dims
     r, c, d = lax.axis_index("row"), lax.axis_index("col"), lax.axis_index("date")
@@ -515,68 +515,59 @@
     wide = n + 256
     f32, bf16 = jnp.float32, jnp.bfloat16
 
-    def plane_peer(k):
-        peer = lax.rem(me + k, n_plane)
-        return peer, (lax.div(peer, n_col), lax.rem(peer, n_col), d)
-
-    def date_peer(k):
-        return (r, c, lax.rem(d + k, n_date))
-
-    def remote_of(src, dst, sems, at, where):
+    def wrapped(value, size):
+        return jnp.where(value >= size, value - size, value)
+
+    plane_peers = []
+    for k in range(1, n_plane):
+        row, col = wrapped(r + k // n_col, n_row), wrapped(c + k % n_col, n_col)
+        plane_peers.append((row * n_col + col, (row, col, d)))
+    date_peers = [(r, c, wrapped(d + k, n_date)) for k in range(1, n_date)]
+
+    def remote_of(src, dst, send_sem, recv_sem, where):
         return pltpu.make_async_remote_copy(
-            src_ref=src, dst_ref=dst, send_sem=sems.at[0, at], recv_sem=sems.at[1, at],
+            src_ref=src, dst_ref=dst, send_sem=send_sem, recv_sem=recv_sem,
             device_id=where, device_id_type=MESH,
         )
 
-    def remote(src, dst, sems, at, where):
-        copy = remote_of(src, dst, sems, at, where)
-        copy.start()
-        return copy
+    def wait_bytes(ref, sem):
+        pltpu.make_async_copy(ref, ref, sem).wait()
 
     barrier = pltpu.get_barrier_semaphore()
-    for k in range(1, n_date):
-        pl.semaphore_signal(barrier, inc=1, device_id=date_peer(k), device_id_type=MESH)
-    for k in range(1, n_plane):
-        pl.semaphore_signal(barrier, inc=1, device_id=plane_peer(k)[1], device_id_type=MESH)
+    for where in date_peers + [where for _, where in plane_peers]:
+        pl.semaphore_signal(barrier, inc=1, device_id=where, device_id_type=MESH)
     fetches = []
     wide_in = zip(
         (idx_any, tgt_any, wl_any, bl_any, wmid_any, bmid_any, wproj_any),
         (idx_in, tgt_in, wl_in, bl_in, wm_in, bm_in, wj_in),
     )
     for k, (src, dst) in enumerate(wide_in):
-        copy = pltpu.make_async_copy(src, dst, w_sem.at[k])
+        copy = pltpu.make_async_copy(src, dst, w_sem.at[min(k, 2)])
         copy.start()
         fetches.append(copy)
     pl.semaphore_wait(barrier, n_plane + n_date - 2)
 
     slab = slc_ref.shape[0]
     chunk = LR * 128
-    down = lax.max(d - 1, 0)
-
-    def own_slab(t):
+    def slab_copy(way, t):
         lanes = pl.ds(t * chunk, chunk)
-        return remote_of(slc_ref.at[:, lanes], pool.at[pl.ds(slab, slab), lanes], slab_sem, t, (r, c, down))
-
-    def far_slab(t):
-        lanes = pl.ds(t * chunk, chunk)
-        return remote_of(
-            pool.at[pl.ds(slab, slab), lanes], pool.at[pl.ds(2 * slab, slab), lanes], slab_sem, tr + t, (r, c, down)
-        )
-
-    has_down = d > 0
-    has_one = d < n_date - 1
-    has_two = d < n_date - 2
-
-    @pl.when(has_down)
-    def _():
-        for t in range(tr):
-            own_slab(t).start()
-
-    @pl.when(jnp.logical_not(has_one))
+        where = (r, c, lax.max(d - way, 0))
+        return remote_of(slc_ref.at[:, lanes], pool.at[pl.ds(way * slab, slab), lanes], slab_sem.at[way - 1], slab_sem.at[2 + (way - 1) * tr + t], where)
+
+    sends = (d > 0, d > 1)
+    gets = (d < n_date - 1, d < n_date - 2)
+    for t in range(tr):
+        for way in (2, 1):
+
+            @pl.when(sends[way - 1])
+            def _():
+                slab_copy(way, t).start()
+
+    @pl.when(jnp.logical_not(gets[0]))
     def _():
         pool[slab : 2 * slab, :] = jnp.zeros((slab, tr * chunk), bf16)
 
-    @pl.when(jnp.logical_not(has_two))
+    @pl.when(jnp.logical_not(gets[1]))
     def _():
         pool[2 * slab : 3 * slab, :] = jnp.zeros((slab, tr * chunk), bf16)
 
@@ -587,7 +578,7 @@
     for ref in (i3a, i3b):
         ref[:, 0:128] = edge
         ref[:, (nb + 1) * 128 : (nb + 2) * 128] = edge
-    x_ref[608:, :] = jnp.zeros((x_ref.shape[0] - 608, 128), f32)
+    x_ref[632:, :] = jnp.zeros((x_ref.shape[0] - 632, 128), f32)
     outs[...] = jnp.zeros_like(outs)
     lane = lax.broadcasted_iota(jnp.int32, (1, 128), 1)
     for copy in fetches[:2]:
@@ -604,7 +595,14 @@
 
     def exchange(src, dst, sems):
         dst[me] = src[me]
-        return [remote(src.at[plane_peer(k)[0]], dst.at[me], sems, k, plane_peer(k)[1]) for k in range(1, n_plane)]
+        for peer, where in plane_peers:
+            remote_of(src.at[peer], dst.at[me], sems.at[0], sems.at[1], where).start()
+
+    def arrived(dst, sems):
+        wait_bytes(dst.at[pl.ds(0, n_plane - 1)], sems.at[1])
+
+    def departed(src, sems):
+        wait_bytes(src.at[pl.ds(0, n_plane - 1)], sems.at[0])
 
     halves = tc * LC // 128
     kinds = 2 * halves
@@ -622,16 +620,7 @@
     avg_lane = lax.broadcasted_iota(jnp.int32, (tc * LC, 128), 1)
     avg = jnp.where(lax.div(spots, LC) + c * tc == avg_lane, 1.0 / (LR * LC), 0.0).astype(f32)
 
-    @pl.when(has_one)
-    def _():
-        for t in range(tr):
-            own_slab(t).wait_recv()
-
-            @pl.when(has_down)
-            def _():
-                far_slab(t).start()
-
-    tgt_copies = exchange(tgt_s, tgt_r, tgt_sem)
+    exchange(tgt_s, tgt_r, tgt_sem)
 
     for copy in fetches[2:]:
         copy.wait()
@@ -672,9 +661,11 @@
 
     for t in range(tr):
 
-        @pl.when(has_two)
-        def _():
-            far_slab(t).wait_recv()
+        for way in (1, 2):
+
+            @pl.when(gets[way - 1])
+            def _():
+                slab_copy(way, t).wait_recv()
 
         picked = mm(pick, pool[:, t * chunk : (t + 1) * chunk])
         sides = []
@@ -694,11 +685,7 @@
             for k in range(pairs):
                 at = z * tr + t
                 look_s[k, at : at + 1, :] = looked[z * pairs + k : z * pairs + k + 1]
-    look_copies = exchange(look_s, look_r, look_sem)
-
-    def settle(copies):
-        for copy in copies:
-            copy.wait_recv()
+    exchange(look_s, look_r, look_sem)
 
     first, last = lane == 0, lane == 127
 
@@ -711,14 +698,14 @@
     def assemble(ref, s):
         return functools.reduce(lambda a, b: a + b, [ref[s * n_col + q] for q in range(n_col)])
 
-    settle(tgt_copies)
+    arrived(tgt_r, tgt_sem)
     for s in range(n_row):
         block = assemble(tgt_r, s)
         for z in range(2):
             for t in range(tr):
                 b = s * tr + t
                 tfld[z : z + 1, b * 128 : (b + 1) * 128] = block[z * tr + t : z * tr + t + 1]
-    settle(look_copies)
+    arrived(look_r, look_sem)
     for s in range(n_row):
         block = assemble(look_r, s)
         for u, turned in enumerate((right(block), block, left(block))):
@@ -773,7 +760,7 @@
                 for t in range(tr):
                     i, b = z * tr + t, s * tr + t
                     outs[s * n_col + q, i : i + 1, :] = shifted[z : z + 1, b * 128 : (b + 1) * 128]
-    den_copies = exchange(outs, den_ref, den_sem)
+    exchange(outs, den_ref, den_sem)
     dn = rounded((tfld[0:2, :] - den) * scale)
     dn3[0:2, 128 : 128 + n] = wide_right(dn)
     dn3[2:4, 128 : 128 + n] = dn
@@ -783,6 +770,36 @@
         grad = mm(wpb_ref[...], taps(dn3, at, 256))
         grad = rounded(jnp.where(h2s[:, at : at + 256].astype(f32) > 0, grad, 0.0))
         turned_store(i3b, grad, at)
+
+    sizes = (192, 192, 192, 64)
+    bases = (0, 192, 384, 576)
+    per = [size // n_plane for size in sizes]
+    count = len(sizes)
+
+    def piece(ref, j, at):
+        return ref.at[pl.ds(pl.multiple_of(bases[j] + at * per[j], 8), per[j])]
+
+    def scatter(j):
+        for k, (peer, where) in enumerate(plane_peers):
+            dst = plane_in.at[j * n_plane + k, pl.ds(0, per[j])]
+            remote_of(piece(x_ref, j, peer), dst, sum_sem.at[0], sum_sem.at[3 + j], where).start()
+
+    def across(j):
+        wait_bytes(plane_in.at[pl.ds(j * n_plane, n_plane - 1), pl.ds(0, per[j])], sum_sem.at[3 + j])
+        part = piece(x_ref, j, me)[...]
+        for k in range(n_plane - 1):
+            part = part + plane_in[j * n_plane + k, 0 : per[j]]
+        slot = date_in.at[j * n_date + d, pl.ds(0, per[j])]
+        slot[...] = part
+        for where in date_peers:
+            remote_of(slot, slot, sum_sem.at[1], sum_sem.at[3 + count + j], where).start()
+
+    def spread(j):
+        wait_bytes(date_in.at[pl.ds(j * n_date, n_date - 1), pl.ds(0, per[j])], sum_sem.at[3 + count + j])
+        mine = piece(o_ref, j, me)
+        mine[...] = functools.reduce(lambda a, b: a + b, [date_in[j * n_date + k, 0 : per[j]] for k in range(n_date)])
+        for _, where in plane_peers:
+            remote_of(mine, mine, sum_sem.at[2], sum_sem.at[3 + 2 * count + j], where).start()
 
     sign = jnp.where(lane < 64, 1.0, -1.0)
     dp2 = i3b[128:256, 128 : 128 + n]
@@ -792,75 +809,46 @@
             upper = gram[u * 128 : u * 128 + 64]
             lower = gram[u * 128 + 64 : u * 128 + 128]
             x_ref[(3 * t + u) * 64 : (3 * t + u) * 64 + 64, :] = upper + sign * pltpu.roll(lower, 64, 1)
-    x_ref[576:600, :] = mm_t(taps(dn3, 0, n), h2s[...])[0:24]
-    x_ref[600:608, :] = mm_t(jnp.ones((16, n), bf16), dp2)[0:8]
-
-    piece = plane_in.shape[1]
-
-    def slot(ref, k):
-        return ref.at[pl.ds(pl.multiple_of(k * piece, 8), piece)]
-
-    scatter = []
-    for k in range(1, n_plane):
-        peer, where = plane_peer(k)
-        scatter.append(remote(slot(x_ref, peer), plane_in.at[k], plane_sem, k, where))
-
-    for at in range(0, n, 256):
+        scatter(t)
+
+    def back1(at):
         h1 = i3a[128:256, at + 128 : at + 384].astype(f32)
         grad = jnp.where(h1 > 0, conv(wb_ref, i3b, at), 0.0)
         dp1[:, at : at + 256] = grad.astype(bf16)
 
-    small_in[me] = mm_t(taps(fld, 0, n), dp1[...])[0:24]
-    small = [
-        remote(small_in.at[me], small_in.at[me], small_sem, k, plane_peer(k)[1]) for k in range(1, n_plane)
-    ]
-    part = slot(x_ref, me)[...]
-    for k, copy in zip(range(1, n_plane), scatter):
-        copy.wait_recv()
-        part = part + plane_in[k]
-    date_in[d] = part
-    spread = [remote(date_in.at[d], date_in.at[d], date_sem, k, date_peer(k)) for k in range(1, n_date)]
-
-    def total(ref, count):
-        return functools.reduce(lambda a, b: a + b, [ref[k] for k in range(count)])
-
-    settle(small)
-    small_date[d] = total(small_in, n_plane)
-    small_spread = [
-        remote(small_date.at[d], small_date.at[d], small_date_sem, k, date_peer(k)) for k in range(1, n_date)
-    ]
-    settle(spread)
-    slot(o_ref, me)[...] = total(date_in, n_date)
-    gather = [
-        remote(slot(o_ref, me), slot(o_ref, me), gather_sem, k, plane_peer(k)[1])
-        for k in range(1, n_plane)
-    ]
-    settle(small_spread)
-    small_ref[...] = total(small_date, n_date)
-    settle(den_copies)
-    settle(gather)
-
-    @pl.when(has_down)
-    def _():
-        for t in range(tr):
-            own_slab(t).wait_send()
-
-    @pl.when(has_down & has_one)
-    def _():
-        for t in range(tr):
-            far_slab(t).wait_send()
-
-    for copy in tgt_copies + look_copies + den_copies + scatter + small + spread + small_spread + gather:
-        copy.wait_send()
-
-
-def whole_finish(dims, den, sums, small, den_out, lift_out, lbias_out, mid_out, mbias_out, proj_out):
+    x_ref[576:600, :] = mm_t(taps(dn3, 0, n), h2s[...])[0:24]
+    x_ref[600:608, :] = mm_t(jnp.ones((16, n), bf16), dp2)[0:8]
+    for at in range(0, n, 256):
+        back1(at)
+    x_ref[608:632, :] = mm_t(taps(fld, 0, n), dp1[...])[0:24]
+    scatter(3)
+    for j in range(count):
+        across(j)
+    for j in range(count):
+        spread(j)
+    arrived(den_ref, den_sem)
+    for j in range(count):
+        wait_bytes(o_ref.at[pl.ds(0, (n_plane - 1) * per[j])], sum_sem.at[3 + 2 * count + j])
+    for way in (1, 2):
+
+        @pl.when(sends[way - 1])
+        def _():
+            wait_bytes(slc_ref, slab_sem.at[way - 1])
+
+    departed(tgt_s, tgt_sem)
+    departed(look_s, look_sem)
+    departed(outs, den_sem)
+    for q, rows in enumerate(((n_plane - 1) * sum(per), (n_date - 1) * sum(per), (n_plane - 1) * sum(per))):
+        wait_bytes(x_ref.at[pl.ds(0, rows)], sum_sem.at[q])
+
+
+def whole_finish(dims, den, sums, den_out, lift_out, lbias_out, mid_out, mbias_out, proj_out):
     n_plane, tr, tc, ch = dims
     for z in range(2):
         for t in range(tr):
             for k in range(n_plane):
                 den_out[z, t, k : k + 1, :] = den[k, z * tr + t : z * tr + t + 1, 0:tc]
-    finish_grads(ch, sums, small, lift_out, lbias_out, mid_out, mbias_out, proj_out)
+    finish_grads(ch, sums, sums.at[608:632], lift_out, lbias_out, mid_out, mbias_out, proj_out)
 
 
 def whole_local(slc, pairs, target, w_lift, b_lift, w_mid, b_mid, w_proj):
@@ -878,20 +866,18 @@
     nb = n_row * tr
     n, wide = nb * 128, (nb + 2) * 128
     n_plane = n_row * n_col
-    piece = -(-608 // (8 * n_plane)) * 8
     zt = -(-2 * tr // 8) * 8
     dma = pltpu.SemaphoreType.DMA
     vmem = pltpu.VMEM
     shape = jax.ShapeDtypeStruct
-    den, sums, small = pl.pallas_call(
+    den, sums = pl.pallas_call(
         functools.partial(whole_kernel, (n_row, n_col, n_date, dates, tr, tc), scale),
         out_shape=(
             shape((n_plane, zt, 128), f32),
-            shape((n_plane * piece, 128), f32),
-            shape((24, 128), f32),
+            shape((640, 128), f32),
         ),
         in_specs=[pl.BlockSpec(memory_space=vmem)] + [pl.BlockSpec(memory_space=pltpu.HBM)] * 7,
-        out_specs=(pl.BlockSpec(memory_space=vmem),) * 3,
+        out_specs=(pl.BlockSpec(memory_space=vmem),) * 2,
         scratch_shapes=[
             vmem((3 * packed.shape[0], packed.shape[1]), bf16),
             vmem((2, count), jnp.int32),
@@ -909,13 +895,13 @@
             vmem((8, wide), f32),
             vmem((2 * ch, n), bf16),
             vmem((n_plane, zt, 128), f32),
-            vmem((n_plane * piece, 128), f32),
+            vmem((640, 128), f32),
             vmem(w_lift.shape, bf16),
             vmem(b_lift.shape, bf16),
             vmem(w_mid.shape, bf16),
             vmem(b_mid.shape, bf16),
             vmem(w_proj.shape, bf16),
-            dma((7,)),
+            dma((3,)),
             vmem((2 * ch, 32), bf16),
             vmem((32, 2 * ch), bf16),
             vmem((2 * ch, 32), bf16),
@@ -923,19 +909,13 @@
             vmem((3, 2 * ch, 6 * ch), bf16),
             vmem((2 * ch, 1), f32),
             vmem((4, 128, 128), f32),
-            vmem((n_plane, piece, 128), f32),
-            vmem((n_date, piece, 128), f32),
-            vmem((n_plane, 24, 128), f32),
-            vmem((n_date, 24, 128), f32),
-            dma((2, n_plane)),
-            dma((2, n_date)),
-            dma((2, 2 * tr)),
-            dma((2, n_plane)),
-            dma((2, n_plane)),
-            dma((2, n_plane)),
-            dma((2, n_plane)),
-            dma((2, n_date)),
-            dma((2, n_plane)),
+            vmem((4 * n_plane, 24, 128), f32),
+            vmem((4 * n_date, 24, 128), f32),
+            dma((2 + 2 * tr,)),
+            dma((2,)),
+            dma((2,)),
+            dma((2,)),
+            dma((15,)),
         ],
         compiler_params=pltpu.CompilerParams(
             collective_id=0, has_side_effects=True, vmem_limit_bytes=48 * 1024 * 1024
@@ -951,10 +931,10 @@
             shape((2, ch), f32),
             shape((3, 3, 2, ch), f32),
         ),
-        in_specs=[pl.BlockSpec(memory_space=vmem)] * 3,
+        in_specs=[pl.BlockSpec(memory_space=vmem)] * 2,
         out_specs=(pl.BlockSpec(memory_space=vmem),) * 6,
         compiler_params=pltpu.CompilerParams(vmem_limit_bytes=8 * 1024 * 1024),
-    )(den, sums, small)
+    )(den, sums)
     return (
         denoised.transpose(0, 2, 1, 3),
         grad_lift.transpose(2, 0, 1, 3),
@@ -965,7 +945,7 @@
     )
 
 
-def local(slc, pairs, target, *weights):
+def local(slc, pairs, target, w_lift, b_lift, w_mid, b_mid, w_proj):
     n_row, n_col = lax.axis_size("row"), lax.axis_size("col")
     count, tr, tc = target.shape[1:]
     whole = (
@@ -974,9 +954,13 @@
         and (n_row * tr) % 2 == 0
         and 2 * tr <= 8
         and count == 8
+        and n_row % 2 == 0
+        and w_mid.shape[-1] == 64
         and (2 * slc.shape[1] * slc.shape[3] // 128) % 16 == 0
     )
-    return (whole_local if whole else halo_local)(slc, pairs, target, *weights)
+    return (whole_local if whole else halo_local)(
+        slc, pairs, target, w_lift, b_lift, w_mid, b_mid, w_proj
+    )
 
 
 def solution(mesh):

time: 38.9 us -> 34.8 us (0.89)
  Pallas kernels: 36 us -> 32.2 us
    pallas_call x1, Pallas kernels: 35 us -> 31.2 us  [whole_local(): pl.pallas_call(functools.partial(whole_kernel, (n_row, n_col, n_date, dat...]
where the time goes in v2:
time: 34.8 us; the launch traced here: 34.6 us
  Pallas kernels  32.2 us (93%)
  local copies, waits for them, and re-layouts  1.69 us (5%)
  between operations  0.73 us (2%)
    pallas_call x1, Pallas kernels, whole_local(): pl.pallas_call(functools.partial(whole_kernel, (n_row, n_col, n_date, dat...  31.2 us
    pallas_call x1, Pallas kernels, whole_local(): pl.pallas_call(functools.partial(whole_finish, (n_plane, tr, tc, ch)), ou...  1.05 us
    reshape x2, local copies, waits for them, and re-layouts, whole_local(): packed = slc.reshape(2, dates, srows, halves, 128).transpose(1, 0, 3, 2, 4)  1 us

profile of v2, /device:TPU:0, one launch (start us, length us, event | category | flops | bytes accessed | tf_op | source)
XLA Modules:
  0.0 34.6 jit_solution(4853823746242212103)
XLA Ops:
  0.6 0.0 copy-start
  0.6 1.0 %reshape.18 = bf16[2,12,6,2,128]{4,3,0,2,1:T(2,128)(2,1)S(1)} reshape(bf16[2,12,6,256]{3,0,2,1:T(2,128)(2,1)} %param.8) | data formatting | bytes 147456 | tf_op jit(solution)/shard_map/reshape | solution.py:861
  1.7 0.0 copy-start.1
  1.7 0.0 copy-start.2
  1.7 0.0 copy-start.3
  1.7 0.0 copy-start.6
  1.7 0.0 copy-start.4
  1.7 0.0 copy-start.5
  1.7 0.0 copy-done
  1.8 0.6 %copy-done.1 = f32[2,8,3,64]{3,1,2,0:T(8,128)S(1)} copy-done((f32[2,8,3,64]{3,1,2,0:T(8,128)S(1)}, f32[2,8,3,64]{3,1,2,0:T(8,128)}, u32[]{:S(2)}) %copy-start.1) | copy-done | bytes 12312
  2.4 0.0 copy-done.2
  2.4 0.0 copy-done.3
  2.4 0.0 copy-done.6
  2.4 0.0 copy-done.4
  2.4 0.0 copy-done.5
  2.4 31.2 %shard_map.127 = (f32[8,8,128]{2,1,0:T(8,128)S(1)}, f32[640,128]{1,0:T(8,128)S(1)}) custom-call(bf16[48,768]{1,0:T(8,128)(2,1)S(1)} %bitcast.15, s32[2,8]{1,0:T(2,128)S(1)} %bitcast.19, f32[2,3,8,64]{3,2,1,0:T(8,128)S(1)} %bitcast.16, bf16[3,3,2,64]{3,2,1,0:T(2,128)(2,1)S(1)} %bitcast.17, bf16[2,64]{1,0:T(2,128)(2,1)S(1)} %copy-done.5, ...), custom_call_target="tpu_custom_call" | custom-call | tf_op jit(solution)/shard_map/pallas_call | solution.py:873
  33.6 1.0 %shard_map.128 = (f32[2,3,8,64]{3,2,1,0:T(8,128)}, f32[3,3,2,64]{3,2,1,0:T(2,128)}, f32[2,64]{1,0:T(2,128)}, f32[2,3,3,64,64]{4,3,2,1,0:T(8,128)}, f32[2,64]{1,0:T(2,128)}, /*index=5*/f32[3,3,2,64]{3,2,1,0:T(2,128)}) custom-call(f32[8,8,128]{2,1,0:T(8,128)S(1)} %get-tuple-element.14.den, f32[640,128]{1,0:T(8,128)S(1)} %get-tuple-element.15.sums), custom_call_target="tpu_custom_call" | custom-call | tf_op jit(solution)/shard_map/pallas_call | solution.py:924
  (2 shorter events, 0.0 us)
Async XLA Ops:
  0.6 1.1 %copy-start = (bf16[2,3,3,64,64]{4,3,2,1,0:T(8,128)(2,1)S(1)}, bf16[2,3,3,64,64]{4,3,2,1,0:T(8,128)(2,1)}, u32[]{:S(2)}) copy-start(bf16[2,3,3,64,64]{4,3,2,1,0:T(8,128)(2,1)} %wmid_any.1) | copy-start | bytes 442372
  1.7 0.7 %copy-start.1 = (f32[2,8,3,64]{3,1,2,0:T(8,128)S(1)}, f32[2,8,3,64]{3,1,2,0:T(8,128)}, u32[]{:S(2)}) copy-start(f32[2,8,3,64]{3,1,2,0:T(8,128)} %param.10) | copy-start | bytes 36868
  1.7 0.7 %copy-start.2 = (bf16[2,3,3,64]{3,0,2,1:T(2,128)(2,1)S(1)}, bf16[2,3,3,64]{3,0,2,1:T(2,128)(2,1)}, u32[]{:S(2)}) copy-start(bf16[2,3,3,64]{3,0,2,1:T(2,128)(2,1)} %param.11) | copy-start | bytes 6916
  1.7 0.7 %copy-start.3 = (bf16[2,3,3,64]{3,0,2,1:T(2,128)(2,1)S(1)}, bf16[2,3,3,64]{3,0,2,1:T(2,128)(2,1)}, u32[]{:S(2)}) copy-start(bf16[2,3,3,64]{3,0,2,1:T(2,128)(2,1)} %param.15) | copy-start | bytes 6916
  1.7 0.7 %copy-start.6 = (bf16[2,64]{1,0:T(2,128)(2,1)S(1)}, bf16[2,64]{1,0:T(2,128)(2,1)}, u32[]{:S(2)}) copy-start(bf16[2,64]{1,0:T(2,128)(2,1)} %bmid_any.1) | copy-start | bytes 772
  1.7 0.7 %copy-start.4 = (s32[8,2]{0,1:T(2,128)S(1)}, s32[8,2]{0,1:T(2,128)}, u32[]{:S(2)}) copy-start(s32[8,2]{0,1:T(2,128)} %param.9) | copy-start | bytes 196
  1.7 0.7 %copy-start.5 = (bf16[2,64]{1,0:T(2,128)(2,1)S(1)}, bf16[2,64]{1,0:T(2,128)(2,1)}, u32[]{:S(2)}) copy-start(bf16[2,64]{1,0:T(2,128)(2,1)} %bl_any.1) | copy-start | bytes 772

commit v3 on v2

--- a/solution.py
+++ b/solution.py
@@ -499,11 +499,11 @@
 
 def whole_kernel(
     dims, scale,
-    slc_ref, idx_any, tgt_any, wl_any, bl_any, wmid_any, bmid_any, wproj_any,
-    den_ref, o_ref,
-    pool, idx_in, tgt_in, look_s, look_r, tgt_s, tgt_r, fld, tfld, i3a, i3b, h2s, tsum, dn3, dp1, outs, x_ref,
+    slc_any, idx_any, tgt_any, wl_any, bl_any, wmid_any, bmid_any, wproj_any,
+    den_ref, o_ref, small_ref,
+    raw, pool, idx_in, tgt_in, look_s, look_r, tgt_s, tgt_r, fld, tfld, i3a, i3b, h2s, tsum, dn3, dp1, outs, x_ref,
     wl_in, bl_in, wm_in, bm_in, wj_in, w_sem, w1_ref, wp_ref, wpb_ref, wf_ref, wb_ref, bm_ref, wtmp,
-    plane_in, date_in, slab_sem, look_sem, tgt_sem, den_sem, sum_sem,
+    plane_in, date_in, small_in, small_date, slab_sem, look_sem, tgt_sem, den_sem, sum_sem, small_sem,
 ):
     n_row, n_col, n_date, dates, tr, tc = dims
     r, c, d = lax.axis_index("row"), lax.axis_index("col"), lax.axis_index("date")
@@ -538,21 +538,25 @@
         pl.semaphore_signal(barrier, inc=1, device_id=where, device_id_type=MESH)
     fetches = []
     wide_in = zip(
-        (idx_any, tgt_any, wl_any, bl_any, wmid_any, bmid_any, wproj_any),
-        (idx_in, tgt_in, wl_in, bl_in, wm_in, bm_in, wj_in),
+        (slc_any, idx_any, tgt_any, wl_any, bl_any, wmid_any, bmid_any, wproj_any),
+        (raw.at[0], idx_in, tgt_in, wl_in, bl_in, wm_in, bm_in, wj_in),
     )
     for k, (src, dst) in enumerate(wide_in):
-        copy = pltpu.make_async_copy(src, dst, w_sem.at[min(k, 2)])
+        copy = pltpu.make_async_copy(src, dst, w_sem.at[min(k, 3)])
         copy.start()
         fetches.append(copy)
     pl.semaphore_wait(barrier, n_plane + n_date - 2)
 
-    slab = slc_ref.shape[0]
+    halves = tc * LC // 128
     chunk = LR * 128
+    depth = pool.shape[0] // (3 * halves)
+
     def slab_copy(way, t):
-        lanes = pl.ds(t * chunk, chunk)
+        rows = pl.ds(t * LR, LR)
         where = (r, c, lax.max(d - way, 0))
-        return remote_of(slc_ref.at[:, lanes], pool.at[pl.ds(way * slab, slab), lanes], slab_sem.at[way - 1], slab_sem.at[2 + (way - 1) * tr + t], where)
+        return remote_of(
+            slc_any.at[:, rows], raw.at[way, :, rows], slab_sem.at[way - 1], slab_sem.at[2 + (way - 1) * tr + t], where
+        )
 
     sends = (d > 0, d > 1)
     gets = (d < n_date - 1, d < n_date - 2)
@@ -563,25 +567,17 @@
             def _():
                 slab_copy(way, t).start()
 
-    @pl.when(jnp.logical_not(gets[0]))
-    def _():
-        pool[slab : 2 * slab, :] = jnp.zeros((slab, tr * chunk), bf16)
-
-    @pl.when(jnp.logical_not(gets[1]))
-    def _():
-        pool[2 * slab : 3 * slab, :] = jnp.zeros((slab, tr * chunk), bf16)
-
-    pool[0:slab, :] = slc_ref[...]
+    pool[...] = jnp.zeros_like(pool)
     for ref in (fld, tfld, dn3, tsum, tgt_s, look_s):
         ref[...] = jnp.zeros_like(ref)
     edge = jnp.zeros((i3a.shape[0], 128), bf16)
     for ref in (i3a, i3b):
         ref[:, 0:128] = edge
         ref[:, (nb + 1) * 128 : (nb + 2) * 128] = edge
-    x_ref[632:, :] = jnp.zeros((x_ref.shape[0] - 632, 128), f32)
+    x_ref[608:, :] = jnp.zeros((x_ref.shape[0] - 608, 128), f32)
     outs[...] = jnp.zeros_like(outs)
     lane = lax.broadcasted_iota(jnp.int32, (1, 128), 1)
-    for copy in fetches[:2]:
+    for copy in fetches[:3]:
         copy.wait()
 
     def to_lane(value):
@@ -604,25 +600,26 @@
     def departed(src, sems):
         wait_bytes(src.at[pl.ds(0, n_plane - 1)], sems.at[0])
 
-    halves = tc * LC // 128
     kinds = 2 * halves
     index = idx_in[...] - d * dates
     spread_lanes = jnp.concatenate([index[0:1]] * kinds + [index[1:2]] * kinds, axis=1)
-    row_of = lax.broadcasted_iota(jnp.int32, (slab, 2 * kinds * pairs), 0)
-    lane_of = lax.broadcasted_iota(jnp.int32, (slab, 2 * kinds * pairs), 1)
-    same_kind = lax.rem(row_of, kinds) == lax.rem(lax.div(lane_of, pairs), kinds)
+    row_of = lax.broadcasted_iota(jnp.int32, (depth * halves, 2 * kinds * pairs), 0)
+    lane_of = lax.broadcasted_iota(jnp.int32, (depth * halves, 2 * kinds * pairs), 1)
+    inner = lax.rem(row_of, depth)
+    kind = lax.rem(inner, 2) * halves + lax.div(row_of, depth)
+    same_kind = (kind == lax.rem(lax.div(lane_of, pairs), kinds)) & (inner < 2 * dates)
     picks = []
     for s in range(3):
-        hit = same_kind & (lax.div(row_of, kinds) + s * dates == spread_lanes)
+        hit = same_kind & (lax.div(inner, 2) + s * dates == spread_lanes)
         picks.append(jnp.where(hit, 1.0, 0.0).astype(f32))
     pick = jnp.concatenate(picks, axis=0).T.astype(bf16)
     spots = lax.broadcasted_iota(jnp.int32, (tc * LC, 128), 0)
     avg_lane = lax.broadcasted_iota(jnp.int32, (tc * LC, 128), 1)
-    avg = jnp.where(lax.div(spots, LC) + c * tc == avg_lane, 1.0 / (LR * LC), 0.0).astype(f32)
+    avg = jnp.where(lax.div(spots, LC) + c * tc == avg_lane, 1.0 / (LR * LC), 0.0).astype(bf16)
 
     exchange(tgt_s, tgt_r, tgt_sem)
 
-    for copy in fetches[2:]:
+    for copy in fetches[3:]:
         copy.wait()
     wtmp[...] = jnp.zeros_like(wtmp)
 
@@ -644,8 +641,9 @@
             wtmp[2, flip + 1 : flip + 2, :] = imag
             wr, wi = wm_in[0, t, u].astype(f32), wm_in[1, t, u].astype(f32)
             block = jnp.concatenate([joined(wr, wi), joined(-wi, wr)], axis=0)
-            wb_ref[2 - t, :, (2 - u) * 128 : (3 - u) * 128] = block.astype(bf16)
-            wf_ref[t, :, u * 128 : (u + 1) * 128] = block.T.astype(bf16)
+            at = (3 * t + u) * 128
+            wb_ref[:, 1024 - at : 1152 - at] = block.astype(bf16)
+            wf_ref[:, at : at + 128] = block.T.astype(bf16)
     bias = bl_in[...].astype(f32)
     wtmp[0, 14:15, :] = joined(bias[0:1], bias[1:2])
     bias = bm_in[...].astype(f32)
@@ -659,13 +657,24 @@
     def rounded(value):
         return value.astype(bf16).astype(f32)
 
+    def pack(way, t):
+        for q in range(LR):
+            for h in range(halves):
+                at = (way * halves + h) * depth
+                lanes = slice((t * LR + q) * 128, (t * LR + q + 1) * 128)
+                pool[at : at + 2 * dates, lanes] = raw[way, :, t * LR + q, :, h * 128 : (h + 1) * 128].reshape(
+                    2 * dates, 128
+                )
+
     for t in range(tr):
-
+        pack(0, t)
+    for t in range(tr):
         for way in (1, 2):
 
             @pl.when(gets[way - 1])
             def _():
                 slab_copy(way, t).wait_recv()
+                pack(way, t)
 
         picked = mm(pick, pool[:, t * chunk : (t + 1) * chunk])
         sides = []
@@ -675,12 +684,13 @@
             for prod in (a0 * b0 + a1 * b1, a1 * b0 - a0 * b1):
                 both.append(sum(prod[:, q * 128 : (q + 1) * 128] for q in range(LR)))
             sides.append(jnp.concatenate(both, axis=0))
-        looked = rounded(
-            jnp.dot(
-                jnp.concatenate(sides, axis=1), avg,
-                precision=lax.Precision.HIGHEST, preferred_element_type=f32,
-            )
-        )
+        summed = jnp.concatenate(sides, axis=1)
+        high = summed.astype(bf16)
+        rest = summed - high.astype(f32)
+        middle = rest.astype(bf16)
+        low = (rest - middle.astype(f32)).astype(bf16)
+        three = mm(jnp.concatenate([high, middle, low], axis=0), avg)
+        looked = rounded(three[0 : 2 * pairs] + (three[2 * pairs : 4 * pairs] + three[4 * pairs :]))
         for z in range(2):
             for k in range(pairs):
                 at = z * tr + t
@@ -727,13 +737,11 @@
 
     for at in range(0, n, 256):
         pre1 = mm(w1_ref[...], taps(fld, at, 256))
-        turned_store(i3a, rounded(jnp.maximum(pre1, 0.0)), at)
+        turned_store(i3a, jnp.maximum(pre1, 0.0), at)
 
     def conv(w_ref, ref, at):
-        total = 0.0
-        for t in range(3):
-            total = total + mm(w_ref[t], ref[:, at + t * 128 : at + t * 128 + 256])
-        return total
+        rows = [ref[:, at + t * 128 : at + t * 128 + 256] for t in range(3)]
+        return mm(w_ref[...], jnp.concatenate(rows, axis=0))
 
     for at in range(0, n, 256):
         pre2 = conv(wf_ref, i3a, at) + bm_ref[...]
@@ -768,11 +776,11 @@
 
     for at in range(0, n, 256):
         grad = mm(wpb_ref[...], taps(dn3, at, 256))
-        grad = rounded(jnp.where(h2s[:, at : at + 256].astype(f32) > 0, grad, 0.0))
+        grad = jnp.where(h2s[:, at : at + 256].astype(f32) > 0, grad, 0.0)
         turned_store(i3b, grad, at)
 
-    sizes = (192, 192, 192, 64)
-    bases = (0, 192, 384, 576)
+    sizes = (192, 192, 256)
+    bases = (0, 192, 384)
     per = [size // n_plane for size in sizes]
     count = len(sizes)
 
@@ -803,29 +811,37 @@
 
     sign = jnp.where(lane < 64, 1.0, -1.0)
     dp2 = i3b[128:256, 128 : 128 + n]
+    x_ref[576:600, :] = mm_t(taps(dn3, 0, n), h2s[...])[0:24]
     for t in range(3):
-        gram = mm_t(i3a[:, t * 128 : t * 128 + n], dp2)
+        rows = i3a[:, t * 128 : t * 128 + n]
+        if t == 2:
+            rows = jnp.concatenate([rows, jnp.ones((16, n), bf16)], axis=0)
+        gram = mm_t(rows, dp2)
         for u in range(3):
             upper = gram[u * 128 : u * 128 + 64]
             lower = gram[u * 128 + 64 : u * 128 + 128]
             x_ref[(3 * t + u) * 64 : (3 * t + u) * 64 + 64, :] = upper + sign * pltpu.roll(lower, 64, 1)
+        if t == 2:
+            x_ref[600:608, :] = gram[384:392]
         scatter(t)
 
-    def back1(at):
+    for at in range(0, n, 256):
         h1 = i3a[128:256, at + 128 : at + 384].astype(f32)
         grad = jnp.where(h1 > 0, conv(wb_ref, i3b, at), 0.0)
         dp1[:, at : at + 256] = grad.astype(bf16)
-
-    x_ref[576:600, :] = mm_t(taps(dn3, 0, n), h2s[...])[0:24]
-    x_ref[600:608, :] = mm_t(jnp.ones((16, n), bf16), dp2)[0:8]
-    for at in range(0, n, 256):
-        back1(at)
-    x_ref[608:632, :] = mm_t(taps(fld, 0, n), dp1[...])[0:24]
-    scatter(3)
+    small_in[me] = mm_t(taps(fld, 0, n), dp1[...])[0:24]
+    for _, where in plane_peers:
+        remote_of(small_in.at[me], small_in.at[me], small_sem.at[0], small_sem.at[1], where).start()
     for j in range(count):
         across(j)
+    wait_bytes(small_in.at[pl.ds(0, n_plane - 1)], small_sem.at[1])
+    small_date[d] = functools.reduce(lambda a, b: a + b, [small_in[k] for k in range(n_plane)])
+    for where in date_peers:
+        remote_of(small_date.at[d], small_date.at[d], small_sem.at[2], small_sem.at[3], where).start()
     for j in range(count):
         spread(j)
+    wait_bytes(small_date.at[pl.ds(0, n_date - 1)], small_sem.at[3])
+    small_ref[...] = functools.reduce(lambda a, b: a + b, [small_date[k] for k in range(n_date)])
     arrived(den_ref, den_sem)
     for j in range(count):
         wait_bytes(o_ref.at[pl.ds(0, (n_plane - 1) * per[j])], sum_sem.at[3 + 2 * count + j])
@@ -833,22 +849,24 @@
 
         @pl.when(sends[way - 1])
         def _():
-            wait_bytes(slc_ref, slab_sem.at[way - 1])
+            wait_bytes(raw.at[0], slab_sem.at[way - 1])
 
     departed(tgt_s, tgt_sem)
     departed(look_s, look_sem)
     departed(outs, den_sem)
+    wait_bytes(small_in.at[pl.ds(0, n_plane - 1)], small_sem.at[0])
+    wait_bytes(small_date.at[pl.ds(0, n_date - 1)], small_sem.at[2])
     for q, rows in enumerate(((n_plane - 1) * sum(per), (n_date - 1) * sum(per), (n_plane - 1) * sum(per))):
         wait_bytes(x_ref.at[pl.ds(0, rows)], sum_sem.at[q])
 
 
-def whole_finish(dims, den, sums, den_out, lift_out, lbias_out, mid_out, mbias_out, proj_out):
+def whole_finish(dims, den, sums, small, den_out, lift_out, lbias_out, mid_out, mbias_out, proj_out):
     n_plane, tr, tc, ch = dims
     for z in range(2):
         for t in range(tr):
             for k in range(n_plane):
                 den_out[z, t, k : k + 1, :] = den[k, z * tr + t : z * tr + t + 1, 0:tc]
-    finish_grads(ch, sums, sums.at[608:632], lift_out, lbias_out, mid_out, mbias_out, proj_out)
+    finish_grads(ch, sums, small, lift_out, lbias_out, mid_out, mbias_out, proj_out)
 
 
 def whole_local(slc, pairs, target, w_lift, b_lift, w_mid, b_mid, w_proj):
@@ -858,8 +876,8 @@
     ch = w_mid.shape[-1]
     halves = scols // 128
     bf16, f32 = jnp.bfloat16, jnp.float32
-    packed = slc.reshape(2, dates, srows, halves, 128).transpose(1, 0, 3, 2, 4)
-    packed = packed.reshape(dates * 2 * halves, srows * 128)
+    images = slc.transpose(1, 2, 0, 3)
+    depth = -(-2 * dates // 16) * 16
     tgt = target.transpose(0, 2, 1, 3)
     w_lift, w_proj = w_lift.transpose(1, 2, 0, 3), w_proj.transpose(1, 2, 0, 3)
     scale = 1.0 / math.sqrt(2.0 * count * n_date * tr * n_row * tc * n_col)
@@ -870,16 +888,22 @@
     dma = pltpu.SemaphoreType.DMA
     vmem = pltpu.VMEM
     shape = jax.ShapeDtypeStruct
-    den, sums = pl.pallas_call(
+    images, index, tgt, w_lift, b_lift, w_mid, b_mid, w_proj = (
+        pltpu.with_memory_space_constraint(x, pltpu.HBM)
+        for x in (images, pairs.T, tgt, w_lift, b_lift, w_mid, b_mid, w_proj)
+    )
+    den, sums, small = pl.pallas_call(
         functools.partial(whole_kernel, (n_row, n_col, n_date, dates, tr, tc), scale),
         out_shape=(
             shape((n_plane, zt, 128), f32),
             shape((640, 128), f32),
+            shape((24, 128), f32),
         ),
-        in_specs=[pl.BlockSpec(memory_space=vmem)] + [pl.BlockSpec(memory_space=pltpu.HBM)] * 7,
-        out_specs=(pl.BlockSpec(memory_space=vmem),) * 2,
+        in_specs=[pl.BlockSpec(memory_space=pltpu.HBM)] * 8,
+        out_specs=(pl.BlockSpec(memory_space=vmem),) * 3,
         scratch_shapes=[
-            vmem((3 * packed.shape[0], packed.shape[1]), bf16),
+            vmem((3,) + images.shape, bf16),
+            vmem((3 * halves * depth, srows * 128), bf16),
             vmem((2, count), jnp.int32),
             vmem(tgt.shape, f32),
             vmem((n_plane, zt, 128), f32),
@@ -901,26 +925,29 @@
             vmem(w_mid.shape, bf16),
             vmem(b_mid.shape, bf16),
             vmem(w_proj.shape, bf16),
-            dma((3,)),
+            dma((4,)),
             vmem((2 * ch, 32), bf16),
             vmem((32, 2 * ch), bf16),
             vmem((2 * ch, 32), bf16),
-            vmem((3, 2 * ch, 6 * ch), bf16),
-            vmem((3, 2 * ch, 6 * ch), bf16),
+            vmem((2 * ch, 18 * ch), bf16),
+            vmem((2 * ch, 18 * ch), bf16),
             vmem((2 * ch, 1), f32),
             vmem((4, 128, 128), f32),
-            vmem((4 * n_plane, 24, 128), f32),
-            vmem((4 * n_date, 24, 128), f32),
+            vmem((3 * n_plane, 32, 128), f32),
+            vmem((3 * n_date, 32, 128), f32),
+            vmem((n_plane, 24, 128), f32),
+            vmem((n_date, 24, 128), f32),
             dma((2 + 2 * tr,)),
             dma((2,)),
             dma((2,)),
             dma((2,)),
-            dma((15,)),
+            dma((12,)),
+            dma((4,)),
         ],
         compiler_params=pltpu.CompilerParams(
             collective_id=0, has_side_effects=True, vmem_limit_bytes=48 * 1024 * 1024
         ),
-    )(packed, pairs.T, tgt, w_lift, b_lift, w_mid, b_mid, w_proj)
+    )(images, index, tgt, w_lift, b_lift, w_mid, b_mid, w_proj)
     denoised, grad_lift, lift_bias, grad_mid, mid_bias, grad_proj = pl.pallas_call(
         functools.partial(whole_finish, (n_plane, tr, tc, ch)),
         out_shape=(
@@ -931,10 +958,10 @@
             shape((2, ch), f32),
             shape((3, 3, 2, ch), f32),
         ),
-        in_specs=[pl.BlockSpec(memory_space=vmem)] * 2,
+        in_specs=[pl.BlockSpec(memory_space=vmem)] * 3,
         out_specs=(pl.BlockSpec(memory_space=vmem),) * 6,
         compiler_params=pltpu.CompilerParams(vmem_limit_bytes=8 * 1024 * 1024),
-    )(den, sums)
+    )(den, sums, small)
     return (
         denoised.transpose(0, 2, 1, 3),
         grad_lift.transpose(2, 0, 1, 3),

time: 34.8 us -> 33.1 us (0.951)
  local copies, waits for them, and re-layouts: 1.69 us -> 0 us
    reshape x2 -> x0, local copies, waits for them, and re-layouts: 1 us -> none  [whole_local(): packed = slc.reshape(2, dates, srows, halves, 128).transpose(1, 0, 3, 2, 4)]
    unnamed x15 -> x0, local copies, waits for them, and re-layouts: 0.69 us -> none
where the time goes in v3:
time: 33.1 us; the launch traced here: 32.9 us
  Pallas kernels  32.3 us (98%)
  between operations  0.64 us (2%)
    pallas_call x1, Pallas kernels, whole_local(): pl.pallas_call(functools.partial(whole_kernel, (n_row, n_col, n_date, dat...  31.2 us
    pallas_call x1, Pallas kernels, whole_local(): pl.pallas_call(functools.partial(whole_finish, (n_plane, tr, tc, ch)), ou...  1.05 us

profile of v3, /device:TPU:0, one launch (start us, length us, event | category | flops | bytes accessed | tf_op | source)
XLA Modules:
  0.0 32.9 jit_solution(2970188538420857483)
XLA Ops:
  0.6 31.2 %shard_map.127 = (f32[8,8,128]{2,1,0:T(8,128)S(1)}, f32[640,128]{1,0:T(8,128)S(1)}, f32[24,128]{1,0:T(8,128)S(1)}) custom-call(bf16[12,6,2,256]{3,2,1,0:T(2,128)(2,1)} %bitcast.8, s32[2,8]{1,0:T(2,128)} %bitcast.12, f32[2,3,8,64]{3,2,1,0:T(8,128)} %bitcast.9, bf16[3,3,2,64]{3,2,1,0:T(2,128)(2,1)} %bitcast.10, bf16[2,64]{1,0:T(2,128)(2,1)} %bl_any.1, ...), custom_call_target="tpu_custom_call" | custom-call | tf_op jit(solution)/shard_map/pallas_call | solution.py:895
  31.9 1.0 %shard_map.128 = (f32[2,3,8,64]{3,2,1,0:T(8,128)}, f32[3,3,2,64]{3,2,1,0:T(2,128)}, f32[2,64]{1,0:T(2,128)}, f32[2,3,3,64,64]{4,3,2,1,0:T(8,128)}, f32[2,64]{1,0:T(2,128)}, /*index=5*/f32[3,3,2,64]{3,2,1,0:T(2,128)}) custom-call(f32[8,8,128]{2,1,0:T(8,128)S(1)} %get-tuple-element.15.den, f32[640,128]{1,0:T(8,128)S(1)} %get-tuple-element.16.sums, ...), custom_call_target="tpu_custom_call" | custom-call | tf_op jit(solution)/shard_map/pallas_call | solution.py:951

commit v4 on v3

--- a/solution.py
+++ b/solution.py
@@ -641,9 +641,8 @@
             wtmp[2, flip + 1 : flip + 2, :] = imag
             wr, wi = wm_in[0, t, u].astype(f32), wm_in[1, t, u].astype(f32)
             block = jnp.concatenate([joined(wr, wi), joined(-wi, wr)], axis=0)
-            at = (3 * t + u) * 128
-            wb_ref[:, 1024 - at : 1152 - at] = block.astype(bf16)
-            wf_ref[:, at : at + 128] = block.T.astype(bf16)
+            wb_ref[(2 - t) * 128 : (3 - t) * 128, (2 - u) * 128 : (3 - u) * 128] = block.astype(bf16)
+            wf_ref[t * 128 : (t + 1) * 128, u * 128 : (u + 1) * 128] = block.T.astype(bf16)
     bias = bl_in[...].astype(f32)
     wtmp[0, 14:15, :] = joined(bias[0:1], bias[1:2])
     bias = bm_in[...].astype(f32)
@@ -700,10 +699,10 @@
     first, last = lane == 0, lane == 127
 
     def right(value):
-        return jnp.where(first, 0.0, pltpu.roll(value, 1, 1))
+        return jnp.where(first, jnp.zeros_like(value), pltpu.roll(value, 1, 1))
 
     def left(value):
-        return jnp.where(last, 0.0, pltpu.roll(value, 127, 1))
+        return jnp.where(last, jnp.zeros_like(value), pltpu.roll(value, 127, 1))
 
     def assemble(ref, s):
         return functools.reduce(lambda a, b: a + b, [ref[s * n_col + q] for q in range(n_col)])
@@ -730,21 +729,30 @@
 
     def turned_store(ref, value, at):
         for q in range(2):
-            piece = value[:, q * 128 : (q + 1) * 128]
+            piece = value[:, q * 128 : (q + 1) * 128].astype(bf16)
             lanes = slice(at + (q + 1) * 128, at + (q + 2) * 128)
             for u, turned in enumerate((right(piece), piece, left(piece))):
-                ref[u * 128 : (u + 1) * 128, lanes] = turned.astype(bf16)
+                ref[u * 128 : (u + 1) * 128, lanes] = turned
 
     for at in range(0, n, 256):
         pre1 = mm(w1_ref[...], taps(fld, at, 256))
         turned_store(i3a, jnp.maximum(pre1, 0.0), at)
 
-    def conv(w_ref, ref, at):
-        rows = [ref[:, at + t * 128 : at + t * 128 + 256] for t in range(3)]
-        return mm(w_ref[...], jnp.concatenate(rows, axis=0))
-
-    for at in range(0, n, 256):
-        pre2 = conv(wf_ref, i3a, at) + bm_ref[...]
+    def conv(w_ref, ref):
+        parts = [mm(w_ref[...], ref[:, at + 128 : at + 384]) for at in range(0, n, 256)]
+        edge = jnp.zeros((128, 128), f32)
+        for p, part in enumerate(parts):
+            above = parts[p - 1][0:128, 128:256] if p else edge
+            below = parts[p + 1][256:384, 0:128] if p + 1 < len(parts) else edge
+            yield (
+                jnp.concatenate([above, part[0:128, 0:128]], axis=1)
+                + part[128:256]
+                + jnp.concatenate([part[256:384, 128:256], below], axis=1)
+            )
+
+    for p, summed in enumerate(conv(wf_ref, i3a)):
+        at = p * 256
+        pre2 = summed + bm_ref[...]
         h2 = jnp.maximum(pre2, 0.0).astype(bf16)
         h2s[:, at : at + 256] = h2
         tsum[:, at + 128 : at + 384] = mm(wp_ref[...], h2)
@@ -825,9 +833,10 @@
             x_ref[600:608, :] = gram[384:392]
         scatter(t)
 
-    for at in range(0, n, 256):
+    for p, summed in enumerate(conv(wb_ref, i3b)):
+        at = p * 256
         h1 = i3a[128:256, at + 128 : at + 384].astype(f32)
-        grad = jnp.where(h1 > 0, conv(wb_ref, i3b, at), 0.0)
+        grad = jnp.where(h1 > 0, summed, 0.0)
         dp1[:, at : at + 256] = grad.astype(bf16)
     small_in[me] = mm_t(taps(fld, 0, n), dp1[...])[0:24]
     for _, where in plane_peers:
@@ -929,8 +938,8 @@
             vmem((2 * ch, 32), bf16),
             vmem((32, 2 * ch), bf16),
             vmem((2 * ch, 32), bf16),
-            vmem((2 * ch, 18 * ch), bf16),
-            vmem((2 * ch, 18 * ch), bf16),
+            vmem((6 * ch, 6 * ch), bf16),
+            vmem((6 * ch, 6 * ch), bf16),
             vmem((2 * ch, 1), f32),
             vmem((4, 128, 128), f32),
             vmem((3 * n_plane, 32, 128), f32),

time: 33.1 us -> 32.3 us (0.976)
  Pallas kernels: 32.3 us -> 31.6 us
    pallas_call x1, Pallas kernels: 31.2 us -> 30.5 us  [whole_local(): pl.pallas_call(functools.partial(whole_kernel, (n_row, n_col, n_date, dat...]
where the time goes in v4:
time: 32.3 us; the launch traced here: 32.2 us
  Pallas kernels  31.6 us (98%)
  between operations  0.64 us (2%)
    pallas_call x1, Pallas kernels, whole_local(): pl.pallas_call(functools.partial(whole_kernel, (n_row, n_col, n_date, dat...  30.5 us
    pallas_call x1, Pallas kernels, whole_local(): pl.pallas_call(functools.partial(whole_finish, (n_plane, tr, tc, ch)), ou...  1.05 us

profile of v4, /device:TPU:0, one launch (start us, length us, event | category | flops | bytes accessed | tf_op | source)
XLA Modules:
  0.0 32.2 jit_solution(1370377033740983515)
XLA Ops:
  0.6 30.5 %shard_map.127 = (f32[8,8,128]{2,1,0:T(8,128)S(1)}, f32[640,128]{1,0:T(8,128)S(1)}, f32[24,128]{1,0:T(8,128)S(1)}) custom-call(bf16[12,6,2,256]{3,2,1,0:T(2,128)(2,1)} %bitcast.8, s32[2,8]{1,0:T(2,128)} %bitcast.12, f32[2,3,8,64]{3,2,1,0:T(8,128)} %bitcast.9, bf16[3,3,2,64]{3,2,1,0:T(2,128)(2,1)} %bitcast.10, bf16[2,64]{1,0:T(2,128)(2,1)} %bl_any.1, ...), custom_call_target="tpu_custom_call" | custom-call | tf_op jit(solution)/shard_map/pallas_call | solution.py:904
  31.1 1.0 %shard_map.128 = (f32[2,3,8,64]{3,2,1,0:T(8,128)}, f32[3,3,2,64]{3,2,1,0:T(2,128)}, f32[2,64]{1,0:T(2,128)}, f32[2,3,3,64,64]{4,3,2,1,0:T(8,128)}, f32[2,64]{1,0:T(2,128)}, /*index=5*/f32[3,3,2,64]{3,2,1,0:T(2,128)}) custom-call(f32[8,8,128]{2,1,0:T(8,128)S(1)} %get-tuple-element.15.den, f32[640,128]{1,0:T(8,128)S(1)} %get-tuple-element.16.sums, ...), custom_call_target="tpu_custom_call" | custom-call | tf_op jit(solution)/shard_map/pallas_call | solution.py:960

commit v5 on v4

--- a/solution.py
+++ b/solution.py
@@ -503,7 +503,7 @@
     den_ref, o_ref, small_ref,
     raw, pool, idx_in, tgt_in, look_s, look_r, tgt_s, tgt_r, fld, tfld, i3a, i3b, h2s, tsum, dn3, dp1, outs, x_ref,
     wl_in, bl_in, wm_in, bm_in, wj_in, w_sem, w1_ref, wp_ref, wpb_ref, wf_ref, wb_ref, bm_ref, wtmp,
-    plane_in, date_in, small_in, small_date, slab_sem, look_sem, tgt_sem, den_sem, sum_sem, small_sem,
+    plane_in, date_in, small_in, small_date, slab_sem, plain_sem, sum_sem,
 ):
     n_row, n_col, n_date, dates, tr, tc = dims
     r, c, d = lax.axis_index("row"), lax.axis_index("col"), lax.axis_index("date")
@@ -519,8 +519,9 @@
         return jnp.where(value >= size, value - size, value)
 
     plane_peers = []
-    for k in range(1, n_plane):
-        row, col = wrapped(r + k // n_col, n_row), wrapped(c + k % n_col, n_col)
+    steps = [(dr, dc) for dr in range(n_row) for dc in range(n_col) if dr or dc]
+    for dr, dc in sorted(steps, key=lambda s: (-min(s[1], n_col - s[1]), -min(s[0], n_row - s[0]))):
+        row, col = wrapped(r + dr, n_row), wrapped(c + dc, n_col)
         plane_peers.append((row * n_col + col, (row, col, d)))
     date_peers = [(r, c, wrapped(d + k, n_date)) for k in range(1, n_date)]
 
@@ -548,6 +549,7 @@
     pl.semaphore_wait(barrier, n_plane + n_date - 2)
 
     halves = tc * LC // 128
+    sent = plain_sem.at[0]
     chunk = LR * 128
     depth = pool.shape[0] // (3 * halves)
 
@@ -555,7 +557,7 @@
         rows = pl.ds(t * LR, LR)
         where = (r, c, lax.max(d - way, 0))
         return remote_of(
-            slc_any.at[:, rows], raw.at[way, :, rows], slab_sem.at[way - 1], slab_sem.at[2 + (way - 1) * tr + t], where
+            slc_any.at[:, rows], raw.at[way, :, rows], sent, slab_sem.at[(way - 1) * tr + t], where
         )
 
     sends = (d > 0, d > 1)
@@ -589,16 +591,13 @@
             for k in range(pairs):
                 tgt_s[k, z * tr + t : z * tr + t + 1, :] = block[k : k + 1]
 
-    def exchange(src, dst, sems):
+    def exchange(src, dst, sem):
         dst[me] = src[me]
         for peer, where in plane_peers:
-            remote_of(src.at[peer], dst.at[me], sems.at[0], sems.at[1], where).start()
-
-    def arrived(dst, sems):
-        wait_bytes(dst.at[pl.ds(0, n_plane - 1)], sems.at[1])
-
-    def departed(src, sems):
-        wait_bytes(src.at[pl.ds(0, n_plane - 1)], sems.at[0])
+            remote_of(src.at[peer], dst.at[me], sent, plain_sem.at[sem], where).start()
+
+    def arrived(dst, sem):
+        wait_bytes(dst.at[pl.ds(0, n_plane - 1)], plain_sem.at[sem])
 
     kinds = 2 * halves
     index = idx_in[...] - d * dates
@@ -617,7 +616,7 @@
     avg_lane = lax.broadcasted_iota(jnp.int32, (tc * LC, 128), 1)
     avg = jnp.where(lax.div(spots, LC) + c * tc == avg_lane, 1.0 / (LR * LC), 0.0).astype(bf16)
 
-    exchange(tgt_s, tgt_r, tgt_sem)
+    exchange(tgt_s, tgt_r, 1)
 
     for copy in fetches[3:]:
         copy.wait()
@@ -673,6 +672,11 @@
             @pl.when(gets[way - 1])
             def _():
                 slab_copy(way, t).wait_recv()
+
+        for way in (1, 2):
+
+            @pl.when(gets[way - 1])
+            def _():
                 pack(way, t)
 
         picked = mm(pick, pool[:, t * chunk : (t + 1) * chunk])
@@ -694,7 +698,7 @@
             for k in range(pairs):
                 at = z * tr + t
                 look_s[k, at : at + 1, :] = looked[z * pairs + k : z * pairs + k + 1]
-    exchange(look_s, look_r, look_sem)
+    exchange(look_s, look_r, 2)
 
     first, last = lane == 0, lane == 127
 
@@ -707,14 +711,14 @@
     def assemble(ref, s):
         return functools.reduce(lambda a, b: a + b, [ref[s * n_col + q] for q in range(n_col)])
 
-    arrived(tgt_r, tgt_sem)
+    arrived(tgt_r, 1)
     for s in range(n_row):
         block = assemble(tgt_r, s)
         for z in range(2):
             for t in range(tr):
                 b = s * tr + t
                 tfld[z : z + 1, b * 128 : (b + 1) * 128] = block[z * tr + t : z * tr + t + 1]
-    arrived(look_r, look_sem)
+    arrived(look_r, 2)
     for s in range(n_row):
         block = assemble(look_r, s)
         for u, turned in enumerate((right(block), block, left(block))):
@@ -776,15 +780,15 @@
                 for t in range(tr):
                     i, b = z * tr + t, s * tr + t
                     outs[s * n_col + q, i : i + 1, :] = shifted[z : z + 1, b * 128 : (b + 1) * 128]
-    exchange(outs, den_ref, den_sem)
+    exchange(outs, den_ref, 3)
     dn = rounded((tfld[0:2, :] - den) * scale)
     dn3[0:2, 128 : 128 + n] = wide_right(dn)
     dn3[2:4, 128 : 128 + n] = dn
     dn3[4:6, 128 : 128 + n] = wide_left(dn)
 
     for at in range(0, n, 256):
-        grad = mm(wpb_ref[...], taps(dn3, at, 256))
-        grad = jnp.where(h2s[:, at : at + 256].astype(f32) > 0, grad, 0.0)
+        grad = mm(wpb_ref[...], taps(dn3, at, 256)).astype(bf16)
+        grad = jnp.where(h2s[:, at : at + 256] > 0, grad, jnp.zeros_like(grad))
         turned_store(i3b, grad, at)
 
     sizes = (192, 192, 256)
@@ -798,24 +802,24 @@
     def scatter(j):
         for k, (peer, where) in enumerate(plane_peers):
             dst = plane_in.at[j * n_plane + k, pl.ds(0, per[j])]
-            remote_of(piece(x_ref, j, peer), dst, sum_sem.at[0], sum_sem.at[3 + j], where).start()
+            remote_of(piece(x_ref, j, peer), dst, sent, sum_sem.at[j], where).start()
 
     def across(j):
-        wait_bytes(plane_in.at[pl.ds(j * n_plane, n_plane - 1), pl.ds(0, per[j])], sum_sem.at[3 + j])
+        wait_bytes(plane_in.at[pl.ds(j * n_plane, n_plane - 1), pl.ds(0, per[j])], sum_sem.at[j])
         part = piece(x_ref, j, me)[...]
         for k in range(n_plane - 1):
             part = part + plane_in[j * n_plane + k, 0 : per[j]]
         slot = date_in.at[j * n_date + d, pl.ds(0, per[j])]
         slot[...] = part
         for where in date_peers:
-            remote_of(slot, slot, sum_sem.at[1], sum_sem.at[3 + count + j], where).start()
+            remote_of(slot, slot, sent, sum_sem.at[count + j], where).start()
 
     def spread(j):
-        wait_bytes(date_in.at[pl.ds(j * n_date, n_date - 1), pl.ds(0, per[j])], sum_sem.at[3 + count + j])
+        wait_bytes(date_in.at[pl.ds(j * n_date, n_date - 1), pl.ds(0, per[j])], sum_sem.at[count + j])
         mine = piece(o_ref, j, me)
         mine[...] = functools.reduce(lambda a, b: a + b, [date_in[j * n_date + k, 0 : per[j]] for k in range(n_date)])
         for _, where in plane_peers:
-            remote_of(mine, mine, sum_sem.at[2], sum_sem.at[3 + 2 * count + j], where).start()
+            remote_of(mine, mine, sent, sum_sem.at[2 * count + j], where).start()
 
     sign = jnp.where(lane < 64, 1.0, -1.0)
     dp2 = i3b[128:256, 128 : 128 + n]
@@ -835,38 +839,37 @@
 
     for p, summed in enumerate(conv(wb_ref, i3b)):
         at = p * 256
-        h1 = i3a[128:256, at + 128 : at + 384].astype(f32)
-        grad = jnp.where(h1 > 0, summed, 0.0)
-        dp1[:, at : at + 256] = grad.astype(bf16)
+        grad = summed.astype(bf16)
+        h1 = i3a[128:256, at + 128 : at + 384]
+        dp1[:, at : at + 256] = jnp.where(h1 > 0, grad, jnp.zeros_like(grad))
     small_in[me] = mm_t(taps(fld, 0, n), dp1[...])[0:24]
     for _, where in plane_peers:
-        remote_of(small_in.at[me], small_in.at[me], small_sem.at[0], small_sem.at[1], where).start()
+        remote_of(small_in.at[me], small_in.at[me], sent, plain_sem.at[4], where).start()
     for j in range(count):
         across(j)
-    wait_bytes(small_in.at[pl.ds(0, n_plane - 1)], small_sem.at[1])
+    wait_bytes(small_in.at[pl.ds(0, n_plane - 1)], plain_sem.at[4])
     small_date[d] = functools.reduce(lambda a, b: a + b, [small_in[k] for k in range(n_plane)])
     for where in date_peers:
-        remote_of(small_date.at[d], small_date.at[d], small_sem.at[2], small_sem.at[3], where).start()
+        remote_of(small_date.at[d], small_date.at[d], sent, plain_sem.at[5], where).start()
     for j in range(count):
         spread(j)
-    wait_bytes(small_date.at[pl.ds(0, n_date - 1)], small_sem.at[3])
+    wait_bytes(small_date.at[pl.ds(0, n_date - 1)], plain_sem.at[5])
     small_ref[...] = functools.reduce(lambda a, b: a + b, [small_date[k] for k in range(n_date)])
-    arrived(den_ref, den_sem)
+    arrived(den_ref, 3)
     for j in range(count):
-        wait_bytes(o_ref.at[pl.ds(0, (n_plane - 1) * per[j])], sum_sem.at[3 + 2 * count + j])
+        wait_bytes(o_ref.at[pl.ds(0, (n_plane - 1) * per[j])], sum_sem.at[2 * count + j])
     for way in (1, 2):
 
         @pl.when(sends[way - 1])
         def _():
-            wait_bytes(raw.at[0], slab_sem.at[way - 1])
-
-    departed(tgt_s, tgt_sem)
-    departed(look_s, look_sem)
-    departed(outs, den_sem)
-    wait_bytes(small_in.at[pl.ds(0, n_plane - 1)], small_sem.at[0])
-    wait_bytes(small_date.at[pl.ds(0, n_date - 1)], small_sem.at[2])
-    for q, rows in enumerate(((n_plane - 1) * sum(per), (n_date - 1) * sum(per), (n_plane - 1) * sum(per))):
-        wait_bytes(x_ref.at[pl.ds(0, rows)], sum_sem.at[q])
+            wait_bytes(raw.at[0], sent)
+
+    for ref in (tgt_s, look_s, outs):
+        wait_bytes(ref.at[pl.ds(0, n_plane - 1)], sent)
+    wait_bytes(small_in.at[pl.ds(0, n_plane - 1)], sent)
+    wait_bytes(small_date.at[pl.ds(0, n_date - 1)], sent)
+    for rows in ((n_plane - 1) * sum(per), (n_date - 1) * sum(per), (n_plane - 1) * sum(per)):
+        wait_bytes(x_ref.at[pl.ds(0, rows)], sent)
 
 
 def whole_finish(dims, den, sums, small, den_out, lift_out, lbias_out, mid_out, mbias_out, proj_out):
@@ -946,12 +949,9 @@
             vmem((3 * n_date, 32, 128), f32),
             vmem((n_plane, 24, 128), f32),
             vmem((n_date, 24, 128), f32),
-            dma((2 + 2 * tr,)),
-            dma((2,)),
-            dma((2,)),
-            dma((2,)),
-            dma((12,)),
-            dma((4,)),
+            dma((2 * tr,)),
+            dma((6,)),
+            dma((9,)),
         ],
         compiler_params=pltpu.CompilerParams(
             collective_id=0, has_side_effects=True, vmem_limit_bytes=48 * 1024 * 1024

time: 32.3 us -> 32.2 us (level)
  no operation moved by 1% of the time
where the time goes in v5:
time: 32.2 us; the launch traced here: 32.1 us
  Pallas kernels  31.4 us (98%)
  between operations  0.64 us (2%)
    pallas_call x1, Pallas kernels, whole_local(): pl.pallas_call(functools.partial(whole_kernel, (n_row, n_col, n_date, dat...  30.4 us
    pallas_call x1, Pallas kernels, whole_local(): pl.pallas_call(functools.partial(whole_finish, (n_plane, tr, tc, ch)), ou...  1.05 us

profile of v5, /device:TPU:0, one launch (start us, length us, event | category | flops | bytes accessed | tf_op | source)
XLA Modules:
  0.0 32.1 jit_solution(6807766447686607205)
XLA Ops:
  0.6 30.4 %shard_map.127 = (f32[8,8,128]{2,1,0:T(8,128)S(1)}, f32[640,128]{1,0:T(8,128)S(1)}, f32[24,128]{1,0:T(8,128)S(1)}) custom-call(bf16[12,6,2,256]{3,2,1,0:T(2,128)(2,1)} %bitcast.8, s32[2,8]{1,0:T(2,128)} %bitcast.12, f32[2,3,8,64]{3,2,1,0:T(8,128)} %bitcast.9, bf16[3,3,2,64]{3,2,1,0:T(2,128)(2,1)} %bitcast.10, bf16[2,64]{1,0:T(2,128)(2,1)} %bl_any.1, ...), custom_call_target="tpu_custom_call" | custom-call | tf_op jit(solution)/shard_map/pallas_call | solution.py:907
  31.0 1.0 %shard_map.128 = (f32[2,3,8,64]{3,2,1,0:T(8,128)}, f32[3,3,2,64]{3,2,1,0:T(2,128)}, f32[2,64]{1,0:T(2,128)}, f32[2,3,3,64,64]{4,3,2,1,0:T(8,128)}, f32[2,64]{1,0:T(2,128)}, /*index=5*/f32[3,3,2,64]{3,2,1,0:T(2,128)}) custom-call(f32[8,8,128]{2,1,0:T(8,128)S(1)} %get-tuple-element.15.den, f32[640,128]{1,0:T(8,128)S(1)} %get-tuple-element.16.sums, ...), custom_call_target="tpu_custom_call" | custom-call | tf_op jit(solution)/shard_map/pallas_call | solution.py:960

commit v6 on v5

--- a/solution.py
+++ b/solution.py
@@ -508,6 +508,8 @@
     n_row, n_col, n_date, dates, tr, tc = dims
     r, c, d = lax.axis_index("row"), lax.axis_index("col"), lax.axis_index("date")
     n_plane = n_row * n_col
+    ch = wm_in.shape[-1]
+    extra = 9 * ch
     me = r * n_col + c
     pairs = n_plane
     nb = n_row * tr
@@ -576,7 +578,7 @@
     for ref in (i3a, i3b):
         ref[:, 0:128] = edge
         ref[:, (nb + 1) * 128 : (nb + 2) * 128] = edge
-    x_ref[608:, :] = jnp.zeros((x_ref.shape[0] - 608, 128), f32)
+    x_ref[extra + 32 :, :] = jnp.zeros((x_ref.shape[0] - extra - 32, 128), f32)
     outs[...] = jnp.zeros_like(outs)
     lane = lax.broadcasted_iota(jnp.int32, (1, 128), 1)
     for copy in fetches[:3]:
@@ -791,8 +793,8 @@
         grad = jnp.where(h2s[:, at : at + 256] > 0, grad, jnp.zeros_like(grad))
         turned_store(i3b, grad, at)
 
-    sizes = (192, 192, 256)
-    bases = (0, 192, 384)
+    sizes = (3 * ch, 3 * ch, 4 * ch)
+    bases = (0, 3 * ch, 6 * ch)
     per = [size // n_plane for size in sizes]
     count = len(sizes)
 
@@ -821,20 +823,20 @@
         for _, where in plane_peers:
             remote_of(mine, mine, sent, sum_sem.at[2 * count + j], where).start()
 
-    sign = jnp.where(lane < 64, 1.0, -1.0)
+    sign = jnp.where(lane < ch, 1.0, -1.0)
     dp2 = i3b[128:256, 128 : 128 + n]
-    x_ref[576:600, :] = mm_t(taps(dn3, 0, n), h2s[...])[0:24]
+    x_ref[extra : extra + 24, :] = mm_t(taps(dn3, 0, n), h2s[...])[0:24]
     for t in range(3):
         rows = i3a[:, t * 128 : t * 128 + n]
         if t == 2:
             rows = jnp.concatenate([rows, jnp.ones((16, n), bf16)], axis=0)
         gram = mm_t(rows, dp2)
         for u in range(3):
-            upper = gram[u * 128 : u * 128 + 64]
-            lower = gram[u * 128 + 64 : u * 128 + 128]
-            x_ref[(3 * t + u) * 64 : (3 * t + u) * 64 + 64, :] = upper + sign * pltpu.roll(lower, 64, 1)
+            upper = gram[u * 128 : u * 128 + ch]
+            lower = gram[u * 128 + ch : u * 128 + 128]
+            x_ref[(3 * t + u) * ch : (3 * t + u + 1) * ch, :] = upper + sign * pltpu.roll(lower, ch, 1)
         if t == 2:
-            x_ref[600:608, :] = gram[384:392]
+            x_ref[extra + 24 : extra + 32, :] = gram[384:392]
         scatter(t)
 
     for p, summed in enumerate(conv(wb_ref, i3b)):
@@ -908,7 +910,7 @@
         functools.partial(whole_kernel, (n_row, n_col, n_date, dates, tr, tc), scale),
         out_shape=(
             shape((n_plane, zt, 128), f32),
-            shape((640, 128), f32),
+            shape((10 * ch, 128), f32),
             shape((24, 128), f32),
         ),
         in_specs=[pl.BlockSpec(memory_space=pltpu.HBM)] * 8,
@@ -931,7 +933,7 @@
             vmem((8, wide), f32),
             vmem((2 * ch, n), bf16),
             vmem((n_plane, zt, 128), f32),
-            vmem((640, 128), f32),
+            vmem((10 * ch, 128), f32),
             vmem(w_lift.shape, bf16),
             vmem(b_lift.shape, bf16),
             vmem(w_mid.shape, bf16),
@@ -945,8 +947,8 @@
             vmem((6 * ch, 6 * ch), bf16),
             vmem((2 * ch, 1), f32),
             vmem((4, 128, 128), f32),
-            vmem((3 * n_plane, 32, 128), f32),
-            vmem((3 * n_date, 32, 128), f32),
+            vmem((3 * n_plane, 4 * ch // n_plane, 128), f32),
+            vmem((3 * n_date, 4 * ch // n_plane, 128), f32),
             vmem((n_plane, 24, 128), f32),
             vmem((n_date, 24, 128), f32),
             dma((2 * tr,)),
@@ -991,7 +993,7 @@
         and 2 * tr <= 8
         and count == 8
         and n_row % 2 == 0
-        and w_mid.shape[-1] == 64
+        and 2 * w_mid.shape[-1] == 128
         and (2 * slc.shape[1] * slc.shape[3] // 128) % 16 == 0
     )
     return (whole_local if whole else halo_local)(

time: 32.2 us -> 32.2 us (level)
  no operation moved by 1% of the time
where the time goes in v6:
time: 32.2 us; the launch traced here: 32.1 us
  Pallas kernels  31.4 us (98%)
  between operations  0.64 us (2%)
    pallas_call x1, Pallas kernels, whole_local(): pl.pallas_call(functools.partial(whole_kernel, (n_row, n_col, n_date, dat...  30.4 us
    pallas_call x1, Pallas kernels, whole_local(): pl.pallas_call(functools.partial(whole_finish, (n_plane, tr, tc, ch)), ou...  1.05 us

profile of v6, /device:TPU:0, one launch (start us, length us, event | category | flops | bytes accessed | tf_op | source)
XLA Modules:
  0.0 32.1 jit_solution(6807766447686607205)
XLA Ops:
  0.6 30.4 %shard_map.127 = (f32[8,8,128]{2,1,0:T(8,128)S(1)}, f32[640,128]{1,0:T(8,128)S(1)}, f32[24,128]{1,0:T(8,128)S(1)}) custom-call(bf16[12,6,2,256]{3,2,1,0:T(2,128)(2,1)} %bitcast.8, s32[2,8]{1,0:T(2,128)} %bitcast.12, f32[2,3,8,64]{3,2,1,0:T(8,128)} %bitcast.9, bf16[3,3,2,64]{3,2,1,0:T(2,128)(2,1)} %bitcast.10, bf16[2,64]{1,0:T(2,128)(2,1)} %bl_any.1, ...), custom_call_target="tpu_custom_call" | custom-call | tf_op jit(solution)/shard_map/pallas_call | solution.py:909
  31.0 1.0 %shard_map.128 = (f32[2,3,8,64]{3,2,1,0:T(8,128)}, f32[3,3,2,64]{3,2,1,0:T(2,128)}, f32[2,64]{1,0:T(2,128)}, f32[2,3,3,64,64]{4,3,2,1,0:T(8,128)}, f32[2,64]{1,0:T(2,128)}, /*index=5*/f32[3,3,2,64]{3,2,1,0:T(2,128)}) custom-call(f32[8,8,128]{2,1,0:T(8,128)S(1)} %get-tuple-element.15.den, f32[640,128]{1,0:T(8,128)S(1)} %get-tuple-element.16.sums, ...), custom_call_target="tpu_custom_call" | custom-call | tf_op jit(solution)/shard_map/pallas_call | solution.py:962
